TPU v7x, 32 devices: a whole 2x2x4 slice. The times are simulated.
32 devices in a mesh: ctx: 16 (over z, y, x), head: 2 (over core).
Axes of the slice: x: 2, y: 2, z: 4, core: 2. Of those that a mesh axis runs over, the one named last changes fastest.
Arguments:
- queries: bfloat16 [2048, 32, 128], P('ctx', 'head'), may hold values from -190 to 190
- keys: bfloat16 [2048, 8, 128], P('ctx', 'head'), may hold values from -6.2 to 6.2
- values: bfloat16 [2048, 8, 128], P('ctx', 'head'), may hold values from -16 to 16
- feature_weight: float32 [32, 128, 128], P('head'), may hold values from -0.5 to 0.5
Outputs:
- student: bfloat16 [2048, 32, 128], P('ctx', 'head')
- update: float32 [32, 128, 128], P('head')
All inputs are finite; a program needn't handle non-finite values.
Results may differ from a plain program's by a relative error of at most 0.003.
The roundings to bfloat16 on the way count: a program that leaves them out, or rounds other values in their place, can miss the bound.
Values may be sent and summed in bfloat16 or wider, within the bound.
A program may use at most 64 MiB of HBM per device.

v0:
```python
import functools
import math

import jax
import jax.numpy as jnp
from jax import lax
from jax.experimental import pallas as pl
from jax.experimental.pallas import tpu as pltpu
from jax.sharding import PartitionSpec as P

precise = lax.Precision.HIGHEST
big_negative = -1e30


def shifted(shard, axis, by):
    devices = lax.axis_size(axis)
    pairs = [(i, i + by) for i in range(devices) if 0 <= i + by < devices]
    return lax.ppermute(shard, axis, pairs)


def carried_in(part, axis, combine, identity):
    count = lax.axis_size(axis)
    place = lax.axis_index(axis)
    ahead = count - 1 - place
    gathered = jax.tree.map(lambda a: lax.all_gather(a, axis), part)
    state = jax.tree.map(lambda a, e: jnp.zeros_like(a) + jnp.asarray(e, a.dtype), part, identity)

    def one(step, state):
        source = count - 1 - step
        return combine(
            state, jax.tree.map(lambda a: lax.dynamic_index_in_dim(a, source, 0, False), gathered)
        )

    return lax.fori_loop(0, ahead, one, state)


def feature_map(projection):
    return jnp.concatenate(
        [jax.nn.softmax(projection, axis=-1), jax.nn.softmax(-projection, axis=-1)], axis=-1
    )


def feature_pull(projection, upstream):
    half_len = upstream.shape[-1] // 2
    upper = jax.nn.softmax(projection, axis=-1)
    lower = jax.nn.softmax(-projection, axis=-1)
    grad_upper = upstream[..., :half_len]
    grad_lower = upstream[..., half_len:]
    upper_part = upper * (grad_upper - jnp.sum(upper * grad_upper, axis=-1, keepdims=True))
    lower_part = lower * (grad_lower - jnp.sum(lower * grad_lower, axis=-1, keepdims=True))
    return upper_part - lower_part


def add_pair(earlier, later):
    return (earlier[0] + later[0], earlier[1] + later[1])


def skip_block(carry_in):
    return carry_in


def general_shards(queries, keys, values, feature_weight):
    block_len, head_count, head_width = queries.shape
    kv_count = keys.shape[1]
    group_size = head_count // kv_count
    feature_len = feature_weight.shape[2] // 2
    my_block = lax.axis_index("ctx")
    score_scale = 1.0 / math.sqrt(head_width)
    grouped_q = queries.reshape(block_len, kv_count, group_size, head_width)
    maps_weight = feature_weight.reshape(kv_count, group_size, head_width, 2 * feature_len)
    query_map = maps_weight[..., :feature_len]
    key_map = maps_weight[..., feature_len:]
    query_pos = my_block * block_len + jnp.arange(block_len, dtype=jnp.int32)
    prev_start = (my_block - 1) * block_len
    last_row = my_block * block_len + block_len - 1
    initial = [
        jnp.full((kv_count, group_size, block_len), big_negative, jnp.float32),
        jnp.zeros((kv_count, group_size, block_len), jnp.float32),
        jnp.zeros((kv_count, group_size, block_len, head_width), jnp.float32),
    ]
    initial = initial + [
        jnp.zeros((kv_count, group_size, 2 * feature_len, head_width), jnp.float32),
        jnp.zeros((kv_count, group_size, 2 * feature_len), jnp.float32),
    ]
    initial = tuple(initial)
    piece_keys = lax.all_gather(keys, "ctx", axis=0, tiled=True)
    piece_values = lax.all_gather(values, "ctx", axis=0, tiled=True)
    piece_rows = piece_keys.shape[0]
    step_rows = math.gcd(piece_rows, 512)

    def attend(step_index, running):
        first_row = step_index * step_rows
        block_keys = lax.dynamic_slice_in_dim(piece_keys, step_index * step_rows, step_rows, 0)
        block_values = lax.dynamic_slice_in_dim(piece_values, step_index * step_rows, step_rows, 0)
        key_pos = first_row + jnp.arange(step_rows, dtype=jnp.int32)

        def compute(carry_in):
            row_max, running_sum, accumulated = (carry_in[0], carry_in[1], carry_in[2])
            scores = (
                jnp.einsum(
                    "tkgd,skd->kgts", grouped_q, block_keys, preferred_element_type=jnp.float32
                )
                * score_scale
            )
            allowed = key_pos[None, :] <= query_pos[:, None]
            scores = jnp.where(allowed, scores, big_negative)
            new_max = jnp.maximum(row_max, jnp.max(scores, axis=-1))
            attn_weight = jnp.where(allowed, jnp.exp(scores - new_max[..., None]), 0.0)
            factor = jnp.exp(row_max - new_max)
            running_sum = running_sum * factor + jnp.sum(attn_weight, axis=-1)
            accumulated = accumulated * factor[..., None] + jnp.einsum(
                "kgts,skd->kgtd",
                attn_weight.astype(jnp.bfloat16),
                block_values,
                preferred_element_type=jnp.float32,
            )
            result = [new_max, running_sum, accumulated] + list(carry_in[3:])
            in_state = (key_pos < prev_start).astype(jnp.float32)
            features = feature_map(
                jnp.einsum(
                    "skd,kgdf->kgsf", block_keys.astype(jnp.float32), key_map, precision=precise
                )
            )
            features = features * in_state[None, None, :, None]
            result[-2] = carry_in[-2] + jnp.einsum(
                "kgsf,skd->kgfd", features, block_values.astype(jnp.float32), precision=precise
            )
            result[-1] = carry_in[-1] + jnp.sum(features, axis=2)
            return tuple(result)

        return lax.cond(first_row <= last_row, compute, skip_block, running)

    folded = lax.fori_loop(0, piece_rows // step_rows, attend, initial)
    teacher = folded[2] / folded[1][..., None]
    stacked = jnp.stack([keys, values])
    moved = shifted(stacked, "ctx", 1)
    prev_keys, prev_values = (moved[0], moved[1])
    has_prev = (my_block > 0).astype(jnp.float32)
    window_keys = jnp.concatenate([prev_keys, keys], axis=0)
    window_values = jnp.concatenate([prev_values, values], axis=0)
    column = jnp.arange(2 * block_len, dtype=jnp.int32)
    row_index = jnp.arange(block_len, dtype=jnp.int32)
    allowed = (column[None, :] < block_len) & (my_block > 0) | (column[None, :] >= block_len) & (
        column[None, :] - block_len <= row_index[:, None]
    )
    scores = (
        jnp.einsum("tkgd,skd->kgts", grouped_q, window_keys, preferred_element_type=jnp.float32)
        * score_scale
    )
    scores = jnp.where(allowed, scores, big_negative)
    row_max = jnp.max(scores, axis=-1)
    window_weight = jnp.where(allowed, jnp.exp(scores - row_max[..., None]), 0.0)
    window_den = jnp.sum(window_weight, axis=-1)
    window_num = jnp.einsum(
        "kgts,skd->kgtd",
        window_weight.astype(jnp.bfloat16),
        window_values,
        preferred_element_type=jnp.float32,
    )
    key_proj = jnp.einsum(
        "skd,kgdf->kgsf", prev_keys.astype(jnp.float32), key_map, precision=precise
    )
    state, norm = (folded[-2], folded[-1])
    query_proj = jnp.einsum(
        "tkgd,kgdf->kgtf", grouped_q.astype(jnp.float32), query_map, precision=precise
    )
    query_feats = feature_map(query_proj)
    decay = jnp.exp(-row_max)
    far_num = decay[..., None] * jnp.einsum(
        "kgtf,kgfd->kgtd", query_feats, state, precision=precise
    )
    far_den = decay * jnp.einsum("kgtf,kgf->kgt", query_feats, norm, precision=precise)
    denominator = window_den + far_den
    mix = (window_num + far_num) / denominator[..., None]
    student = jnp.transpose(mix.astype(jnp.bfloat16), (2, 0, 1, 3)).reshape(
        block_len, head_count, head_width
    )
    mismatch = mix - teacher
    grad_num = mismatch / denominator[..., None]
    grad_den = -jnp.sum(mismatch * mix, axis=-1) / denominator
    lifted = decay[..., None] * query_feats
    grad_state = jnp.einsum("kgtf,kgtd->kgfd", lifted, grad_num, precision=precise)
    grad_norm = jnp.einsum("kgtf,kgt->kgf", lifted, grad_den, precision=precise)
    grad_qfeat = decay[..., None] * (
        jnp.einsum("kgfd,kgtd->kgtf", state, grad_num, precision=precise)
        + norm[:, :, None, :] * grad_den[..., None]
    )
    later_state, later_norm = carried_in(
        (grad_state, grad_norm),
        "ctx",
        add_pair,
        (jnp.zeros_like(grad_state), jnp.zeros_like(grad_norm)),
    )
    grad_kfeat = (
        jnp.einsum(
            "kgfd,skd->kgsf", later_state, prev_values.astype(jnp.float32), precision=precise
        )
        + later_norm[:, :, None, :]
    ) * has_prev
    grad_query = jnp.einsum(
        "tkgd,kgtf->kgdf",
        grouped_q.astype(jnp.float32),
        feature_pull(query_proj, grad_qfeat),
        precision=precise,
    )
    grad_key = jnp.einsum(
        "skd,kgsf->kgdf",
        prev_keys.astype(jnp.float32),
        feature_pull(key_proj, grad_kfeat),
        precision=precise,
    )
    gradients = jnp.concatenate([grad_query, grad_key], axis=-1).reshape(
        head_count, head_width, 2 * feature_len
    )
    entry_count = gradients.size * lax.axis_size("head")
    summed = lax.psum(gradients, "ctx")
    squares = lax.psum(jnp.sum(summed * summed), "head")
    update = summed / jnp.sqrt(squares / entry_count + 1e-06)
    return (student, update)


f32, bf16 = jnp.float32, jnp.bfloat16
NN = (((1,), (0,)), ((), ()))
NT = (((1,), (1,)), ((), ()))
TN = (((0,), (0,)), ((), ()))


def mxu(a, b, dims):
    return lax.dot_general(a, b, dims, preferred_element_type=f32)


def split(x, pieces):
    out = []
    for _ in range(pieces):
        piece = x.astype(bf16)
        out.append(piece)
        x = x - piece.astype(f32)
    return out


def cat(parts, axis):
    return jnp.concatenate(parts, axis=axis)


def exact_by_wide(a, b, dims):
    return mxu(cat([a, a], dims[0][0][0]), cat(split(b, 2), dims[0][1][0]), dims)


def wide_by_exact(a, b, dims):
    return mxu(cat(split(a, 2), dims[0][0][0]), cat([b, b], dims[0][1][0]), dims)


def wide_by_wide(a, b, dims):
    a_hi, a_lo = split(a, 2)
    b_hi, b_lo = split(b, 2)
    return mxu(
        cat([a_hi, a_hi, a_lo], dims[0][0][0]), cat([b_hi, b_lo, b_hi], dims[0][1][0]), dims
    )


def half_sum(x, halves):
    return wide_by_exact(x, halves, NN)


def half_softmax(u, is_upper, halves):
    top = jnp.max(jnp.where(is_upper, u, big_negative), axis=-1, keepdims=True)
    low = jnp.max(jnp.where(is_upper, big_negative, u), axis=-1, keepdims=True)
    e = jnp.exp(u - jnp.where(is_upper, top, low))
    return e / half_sum(e, halves)


def remote(src, dst, send_sem, recv_sem, **where):
    return pltpu.make_async_remote_copy(
        src_ref=src,
        dst_ref=dst,
        send_sem=send_sem,
        recv_sem=recv_sem,
        device_id=where,
        device_id_type=pl.DeviceIdType.MESH,
    )


def each(count, body):
    def step(index, carry):
        body(index)
        return carry

    lax.fori_loop(0, count, step, 0)


def head_kernel(
    qt_ref, kvt_ref, w_ref, student_ref, update_ref,
    q_all, kv_all, mix_ref, gat_ref, gat_key_ref, sq_ref, own_ref, sum_ref, pre_ref, pre_norm_ref,
    score_ref, kfeat_ref, gstate_ref, gnorm_ref, state_ref, norm_ref,
    wq_ref, wk_ref, acc_ref, peak_ref, total_ref, gq_ref, gk_ref,
    q_send, q_recv, kv_send, kv_recv, kv_relay, local_sem, st_send, st_recv,
    g_send, g_relay, g_recv, sq_send, sq_recv,
):
    blocks, length, width = qt_ref.shape
    planes = kvt_ref.shape[0]
    group = blocks // planes
    me, side = lax.axis_index("ctx"), lax.axis_index("head")
    plane, spot = me // group, me % group
    features = w_ref.shape[1] // 2
    rows = 2 * length
    steps = blocks // 2

    gats = (gat_ref, gat_key_ref)
    barrier = pltpu.get_barrier_semaphore()

    def greet(t):
        @pl.when(t != me)
        def _():
            pl.semaphore_signal(
                barrier, inc=1, device_id={"ctx": t}, device_id_type=pl.DeviceIdType.MESH
            )

    each(blocks, greet)
    pl.semaphore_signal(
        barrier, inc=1, device_id={"head": 1 - side}, device_id_type=pl.DeviceIdType.MESH
    )
    pl.semaphore_wait(barrier, blocks)

    def kv_column(g):
        return remote(
            kvt_ref.at[g], kv_all.at[me], kv_send.at[g], kv_recv.at[me], ctx=g * group + spot
        )

    def kv_own(r):
        return remote(
            kvt_ref.at[plane], kv_all.at[me], kv_relay.at[plane, r], kv_recv.at[me],
            ctx=plane * group + r,
        )

    def kv_pass(z, r):
        block = z * group + spot
        return remote(
            kv_all.at[block], kv_all.at[block], kv_relay.at[z, r], kv_recv.at[block],
            ctx=plane * group + r,
        )

    def q_copy(t):
        return remote(qt_ref.at[t], q_all.at[me], q_send.at[t], q_recv.at[me], ctx=t)

    def q_arrival(b):
        return remote(qt_ref.at[b], q_all.at[b], q_send.at[b], q_recv.at[b], ctx=b)

    def kv_arrival(b):
        return remote(
            kv_all.at[b], kv_all.at[b], kv_send.at[0], kv_recv.at[b], ctx=b
        )

    def st_copy(b):
        return remote(mix_ref.at[b], student_ref.at[me], st_send.at[b], st_recv.at[me], ctx=b)

    def st_arrival(b):
        return remote(mix_ref.at[b], student_ref.at[b], st_send.at[b], st_recv.at[b], ctx=b)

    def g_column(part, z):
        piece = gats[part].at[me]
        return remote(
            piece, piece, g_send.at[part, z], g_recv.at[me, part], ctx=z * group + spot
        )

    def g_pass(part, z, r):
        block = z * group + spot
        piece = gats[part].at[block]
        return remote(
            piece, piece, g_relay.at[part, z, r], g_recv.at[block, part], ctx=plane * group + r
        )

    def g_arrival(part, b):
        piece = gats[part].at[b]
        return remote(piece, piece, g_send.at[part, 0], g_recv.at[b, part], ctx=b)

    def planes_but_mine(body):
        def one(z):
            @pl.when(z != plane)
            def _():
                body(z)

        each(planes, one)

    def spots_but_mine(body):
        def one(r):
            @pl.when(r != spot)
            def _():
                body(r)

        each(group, one)

    planes_but_mine(lambda g: kv_column(g).start())
    spots_but_mine(lambda r: kv_own(r).start())
    own_kv = pltpu.make_async_copy(kvt_ref.at[plane], kv_all.at[me], local_sem.at[0])
    own_q = pltpu.make_async_copy(qt_ref.at[me], q_all.at[me], local_sem.at[1])
    own_kv.start()
    own_q.start()
    scale = 1.0 / math.sqrt(width)
    lane = lax.broadcasted_iota(jnp.int32, (rows, 2 * features), 1)
    is_upper = lane < features
    row_half = lax.broadcasted_iota(jnp.int32, (2 * features, 2 * features), 0) < features
    col_half = lax.broadcasted_iota(jnp.int32, (2 * features, 2 * features), 1) < features
    halves = jnp.where(row_half == col_half, 1.0, 0.0).astype(bf16)
    w = w_ref[...]
    wq, wk = w[:, :features], w[:, features:]
    wq_ref[...] = cat(split(cat([wq, -wq], 1), 3), 0)
    wk_ref[...] = cat(split(cat([wk, -wk], 1), 3), 0)
    for ref in (state_ref, norm_ref, gq_ref, gk_ref):
        ref[...] = jnp.zeros_like(ref)
    own_kv.wait()
    own_q.wait()

    def pass_on(z):
        kv_arrival(z * group + spot).wait_recv()
        spots_but_mine(lambda r: kv_pass(z, r).start())


    def load(part, i):
        if part == 0:
            return q_all[pl.ds(2 * i, 2)].reshape(rows, width)
        return kv_all[pl.ds(2 * i, 2), part - 1].reshape(rows, width)

    def q_arrived(b):
        @pl.when(b != me)
        def _():
            q_arrival(b).wait_recv()

    def kv_arrived(b):
        @pl.when(b % group != spot)
        def _():
            kv_arrival(b).wait_recv()

    def send_student(b):
        @pl.when(b != me)
        def _():
            st_copy(b).start()

        @pl.when(b == me)
        def _():
            student_ref[me] = mix_ref[me]

    def send_grad(part):
        planes_but_mine(lambda z: g_column(part, z).start())
        spots_but_mine(lambda r: g_pass(part, plane, r).start())

    def relay_grad(part):
        def one(z):
            g_arrival(part, z * group + spot).wait_recv()
            spots_but_mine(lambda r: g_pass(part, z, r).start())

        planes_but_mine(one)

    def key_side(i):
        kv_arrived(2 * i)
        kv_arrived(2 * i + 1)
        k, v = load(1, i), load(2, i)
        kf = half_softmax(mxu(cat([k, k, k], 1), wk_ref[...], NN), is_upper, halves)
        kfeat_ref[i] = kf
        own_ref[2 * i] = wide_by_exact(kf[:length], v[:length], TN)
        own_ref[2 * i + 1] = wide_by_exact(kf[length:], v[length:], TN)
        sum_ref[2 * i] = jnp.sum(kf[:length], axis=0, keepdims=True)
        sum_ref[2 * i + 1] = jnp.sum(kf[length:], axis=0, keepdims=True)

    def push(d):
        q_copy((me + 2 * blocks - 1 - d) % blocks).start()

    each(blocks - 1, push)

    def relay_first(dz):
        pass_on((plane + dz + 1) % planes)

    each(planes - 1, relay_first)

    def stage(dz):
        half = group // 2
        each(half, lambda u: key_side((plane + dz) % planes * half + u))

    each(planes, stage)
    for b in range(2):
        pre_ref[b] = jnp.zeros_like(pre_ref[b])
        pre_norm_ref[b] = jnp.zeros_like(pre_norm_ref[b])

    def prefix(b):
        pre_ref[b + 2] = pre_ref[b + 1] + own_ref[b]
        pre_norm_ref[b + 2] = pre_norm_ref[b + 1] + sum_ref[b]

    each(blocks - 2, prefix)

    def forward(turn, carry):
        i = (me // 2 + turn) % steps
        q_arrived(2 * i)
        q_arrived(2 * i + 1)
        q, v = load(0, i), load(2, i)
        acc_ref[...] = jnp.zeros_like(acc_ref)
        total_ref[...] = jnp.zeros_like(total_ref)
        peak_ref[...] = jnp.full(peak_ref.shape, big_negative, f32)

        def pair_of(part, j):
            return cat([load(part, 2 * j), load(part, 2 * j + 1)], 0)

        def keep(j, s):
            score_ref[2 * j] = s[:, :rows]
            score_ref[2 * j + 1] = s[:, rows:]
            top = jnp.maximum(s[:, :rows], s[:, rows:])
            peak_ref[...] = jnp.maximum(
                peak_ref[...], jnp.maximum(top[:, :length], top[:, length:])
            )

        last = i // 2
        each(last, lambda j: keep(j, mxu(q, pair_of(1, j), NT) * scale))
        s = mxu(q, pair_of(1, last), NT) * scale
        column = lax.broadcasted_iota(jnp.int32, (rows, 2 * rows), 1)
        row = lax.broadcasted_iota(jnp.int32, (rows, 2 * rows), 0)
        keep(last, jnp.where(column <= row + (i - 2 * last) * rows, s, big_negative))
        row_max = jnp.max(peak_ref[...], axis=-1, keepdims=True)

        def weigh(j):
            p0 = jnp.exp(score_ref[2 * j] - row_max)
            p1 = jnp.exp(score_ref[2 * j + 1] - row_max)
            both = p0 + p1
            total_ref[...] += both[:, :length] + both[:, length:]
            p = cat([p0.astype(bf16), p1.astype(bf16)], 1)
            acc_ref[...] += mxu(p, pair_of(2, j), NN)

        each(last + 1, weigh)
        teacher = acc_ref[...] / jnp.sum(total_ref[...], axis=-1, keepdims=True)

        before = jnp.maximum(i - 1, 0)
        s = score_ref[i]
        prev_top = score_ref[before, :length, length:]
        prev_top = jnp.where(i > 0, prev_top, big_negative)
        prev = cat([prev_top, s[length:, :length]], 0)
        own = cat([s[:length, :length], s[length:, length:]], 0)
        win_max = jnp.max(jnp.maximum(prev, own), axis=-1, keepdims=True)
        p_prev, p_own = jnp.exp(prev - win_max), jnp.exp(own - win_max)
        win_den = jnp.sum(p_prev + p_own, axis=-1, keepdims=True)
        b_prev, b_own = p_prev.astype(bf16), p_own.astype(bf16)
        v_before = kv_all[jnp.maximum(2 * i - 1, 0), 1]
        win_num = cat(
            [
                mxu(cat([b_prev[:length], b_own[:length]], 1), cat([v_before, v[:length]], 0), NN),
                mxu(cat([b_prev[length:], b_own[length:]], 1), v, NN),
            ],
            0,
        )

        qf = half_softmax(mxu(cat([q, q, q], 1), wq_ref[...], NN), is_upper, halves)
        state_0, norm_0 = pre_ref[2 * i], pre_norm_ref[2 * i]
        state_1, norm_1 = pre_ref[2 * i + 1], pre_norm_ref[2 * i + 1]

        norm = cat(
            [
                jnp.broadcast_to(norm_0, (length, 2 * features)),
                jnp.broadcast_to(norm_1, (length, 2 * features)),
            ],
            0,
        )
        decay = jnp.exp(-win_max)
        far = cat(
            [wide_by_wide(qf[:length], state_0, NN), wide_by_wide(qf[length:], state_1, NN)], 0
        )
        den = win_den + decay * jnp.sum(qf * norm, axis=-1, keepdims=True)
        mix = (win_num + decay * far) / den
        mix_ref[pl.ds(2 * i, 2)] = mix.astype(bf16).reshape(2, length, width)
        send_student(2 * i)
        send_student(2 * i + 1)
        mismatch = mix - teacher
        g_num = mismatch / den
        g_den = -jnp.sum(mismatch * mix, axis=-1, keepdims=True) / den
        lifted = decay * qf
        gstate_ref[2 * i] = wide_by_wide(lifted[:length], g_num[:length], TN)
        gstate_ref[2 * i + 1] = wide_by_wide(lifted[length:], g_num[length:], TN)
        pulled_norm = lifted * g_den
        gnorm_ref[2 * i] = jnp.sum(pulled_norm[:length], axis=0, keepdims=True)
        gnorm_ref[2 * i + 1] = jnp.sum(pulled_norm[length:], axis=0, keepdims=True)
        g_qf = decay * (
            cat(
                [
                    wide_by_wide(g_num[:length], state_0, NT),
                    wide_by_wide(g_num[length:], state_1, NT),
                ],
                0,
            )
            + norm * g_den
        )
        d_q = qf * (g_qf - half_sum(qf * g_qf, halves))
        gq_ref[...] += wide_by_exact(d_q, q, TN)
        return carry

    lax.fori_loop(0, steps, forward, 0)
    gat_ref[me] = (gq_ref[:features] - gq_ref[features:]).astype(bf16)
    send_grad(0)

    for ref in (state_ref, norm_ref):
        ref[...] = jnp.zeros_like(ref)

    def backward(step, carry):
        i = steps - 1 - step
        k, v, kf = load(1, i), load(2, i), kfeat_ref[i]
        nxt = jnp.minimum(i + 1, steps - 1)
        live = jnp.where(step > 0, 1.0, 0.0)
        later_1, later_n1 = state_ref[...], norm_ref[...]
        later_0 = later_1 + live * gstate_ref[2 * nxt]
        later_n0 = later_n1 + live * gnorm_ref[2 * nxt]
        g_kf = cat(
            [
                exact_by_wide(v[:length], later_0, NT) + later_n0,
                exact_by_wide(v[length:], later_1, NT) + later_n1,
            ],
            0,
        )
        d_k = kf * (g_kf - half_sum(kf * g_kf, halves))
        gk_ref[...] += wide_by_exact(d_k, k, TN)
        state_ref[...] = later_0 + gstate_ref[2 * i + 1]
        norm_ref[...] = later_n0 + gnorm_ref[2 * i + 1]
        return carry

    lax.fori_loop(0, steps, backward, 0)
    gat_key_ref[me] = (gk_ref[:features] - gk_ref[features:]).astype(bf16)
    send_grad(1)
    relay_grad(0)
    relay_grad(1)

    def gathered(b):
        @pl.when(b % group != spot)
        def _():
            g_arrival(0, b).wait_recv()
            g_arrival(1, b).wait_recv()

    each(blocks, gathered)
    squares = jnp.zeros((8, width), f32)
    for b in range(blocks):
        piece = cat([gat_ref[b], gat_key_ref[b]], 0).astype(f32)
        piece = piece.reshape(2 * features // 8, 8, width)
        squares = squares + jnp.sum(piece * piece, axis=0)
    sq_ref[0] = squares
    swap = remote(sq_ref.at[0], sq_ref.at[1], sq_send.at[0], sq_recv.at[0], head=1 - side)
    swap.start()

    def turned(b):
        update_ref[b] = cat([gat_ref[b], gat_key_ref[b]], 0).astype(f32).T

    each(blocks, turned)

    def settle(t):
        @pl.when(t != me)
        def _():
            q_copy(t).wait_send()
            st_copy(t).wait_send()
            st_arrival(t).wait_recv()

    each(blocks, settle)

    def settle_plane(z):
        @pl.when(z != plane)
        def _():
            kv_column(z).wait_send()
            g_column(0, z).wait_send()
            g_column(1, z).wait_send()

        def one(r):
            kv_pass(z, r).wait_send()
            g_pass(0, z, r).wait_send()
            g_pass(1, z, r).wait_send()

        spots_but_mine(one)

    each(planes, settle_plane)
    swap.wait()
    entries = 2 * blocks * width * 2 * features
    total = jnp.sum(sq_ref[0] + sq_ref[1], keepdims=True)
    inverse = 1.0 / jnp.sqrt(total / entries + 1e-06)

    def scaled(b):
        update_ref[b] = update_ref[b] * inverse

    each(blocks, scaled)


def whole_head(qt, kvt, w):
    blocks, length, width = qt.shape
    planes = kvt.shape[0]
    group = blocks // planes
    double = w.shape[1]
    rows, steps = 2 * length, blocks // 2
    vmem, dma = pltpu.VMEM, pltpu.SemaphoreType.DMA
    return pl.pallas_call(
        head_kernel,
        out_shape=(
            jax.ShapeDtypeStruct((blocks, length, width), bf16),
            jax.ShapeDtypeStruct((blocks, width, double), f32),
        ),
        in_specs=[pl.BlockSpec(memory_space=vmem)] * 3,
        out_specs=(pl.BlockSpec(memory_space=vmem),) * 2,
        scratch_shapes=[
            vmem((blocks, length, width), bf16),
            vmem((blocks, 2, length, width), bf16),
            vmem((blocks, length, width), bf16),
            vmem((blocks, double // 2, width), bf16),
            vmem((blocks, double // 2, width), bf16),
            vmem((2, 8, width), f32),
            vmem((blocks, double, width), f32),
            vmem((blocks, 1, double), f32),
            vmem((blocks, double, width), f32),
            vmem((blocks, 1, double), f32),
            vmem((steps, rows, rows), f32),
            vmem((steps, rows, double), f32),
            vmem((blocks, double, width), f32),
            vmem((blocks, 1, double), f32),
            vmem((double, width), f32),
            vmem((1, double), f32),
            vmem((3 * width, double), bf16),
            vmem((3 * width, double), bf16),
            vmem((rows, width), f32),
            vmem((rows, length), f32),
            vmem((rows, length), f32),
            vmem((double, width), f32),
            vmem((double, width), f32),
            dma((blocks,)),
            dma((blocks,)),
            dma((planes,)),
            dma((blocks,)),
            dma((planes, group)),
            dma((2,)),
            dma((blocks,)),
            dma((blocks,)),
            dma((2, planes)),
            dma((2, planes, group)),
            dma((blocks, 2)),
            dma((1,)),
            dma((1,)),
        ],
        compiler_params=pltpu.CompilerParams(
            vmem_limit_bytes=40 * 2**20, collective_id=0, has_side_effects=True
        ),
    )(qt, kvt, w)


def head_shards(queries, keys, values, feature_weight):
    qt = jnp.transpose(queries, (1, 0, 2))
    kvt = jnp.transpose(jnp.stack([keys, values]), (2, 0, 1, 3))
    w = lax.dynamic_index_in_dim(feature_weight, lax.axis_index("ctx"), 0, False)
    student, update = whole_head(qt, kvt, w)
    return (jnp.transpose(student, (1, 0, 2)), update)


def shards(queries, keys, values, feature_weight):
    count = lax.axis_size("ctx")
    width = queries.shape[2]
    fits = queries.shape[1] == count and lax.axis_size("head") == 2 and count % 4 == 0 and count * queries.shape[0] <= 4096
    fits = fits and queries.shape[1] // keys.shape[1] % 2 == 0 and queries.shape[0] == width and feature_weight.shape[2] == width
    body = head_shards if fits else general_shards
    return body(queries, keys, values, feature_weight)


def solution(mesh):
    return jax.shard_map(
        shards,
        mesh=mesh,
        in_specs=(
            P("ctx", "head", None),
            P("ctx", "head", None),
            P("ctx", "head", None),
            P("head", None, None),
        ),
        out_specs=(P("ctx", "head", None), P("head", None, None)),
        check_vma=False,
    )
```

profile of v0, /device:TPU:0, one launch (start us, length us, event | category | flops | bytes accessed | tf_op | source)
XLA Modules:
  0.0 70.7 jit_solution(11952156818924180778)
XLA Ops:
  0.6 0.0 copy-start
  0.6 0.0 copy-start.2
  0.7 1.2 %copy-done = f32[16,128,128]{2,1,0:T(8,128)S(1)} copy-done((f32[16,128,128]{2,1,0:T(8,128)S(1)}, f32[16,128,128]{2,1,0:T(8,128)}, u32[]{:S(2)}) %copy-start) | copy-done | bytes 1048600
  1.9 0.0 copy-done.2
  1.9 0.0 copy-start.1
  1.9 1.0 %copy_bitcast_fusion.1 = (bf16[1,128,4,128]{3,1,0,2:T(8,128)(2,1)S(1)}, bf16[1,128,4,128]{3,1,0,2:T(8,128)(2,1)S(1)}) fusion(bf16[128,4,128]{2,1,0:T(4,128)(2,1)S(1)} %copy-done.2, bf16[128,4,128]{2,1,0:T(4,128)(2,1)} %param.5), kind=kLoop, calls=%fused_computation.2 | loop fusion | bytes 524288 | tf_op jit(solution)/shard_map/stack | solution.py:741
  2.9 0.1 copy-done.1
  3.0 0.1 copy.13
  3.1 65.4 %shard_map.59 = (bf16[16,128,128]{2,1,0:T(8,128)(2,1)S(1)}, f32[16,128,128]{2,1,0:T(8,128)S(1)}) custom-call(bf16[16,128,128]{2,1,0:T(8,128)(2,1)S(1)} %bitcast.12, bf16[4,2,128,128]{3,2,1,0:T(8,128)(2,1)S(1)} %maximum_bitcast_fusion.kvt_ref, f32[128,128]{1,0:T(8,128)S(1)} %dynamic-slice_bitcast_fusion.w_ref), custom_call_target="tpu_custom_call" | custom-call | tf_op jit(solution)/shard_map/pallas_call | solution.py:687
  68.6 1.1 %copy.9 = bf16[128,16,128]{2,1,0:T(8,128)(2,1)} copy(bf16[128,16,128]{2,0,1:T(8,128)(2,1)S(1)} %bitcast.13) | data formatting | bytes 1048576
  69.7 1.0 %copy.15 = f32[16,128,128]{2,1,0:T(8,128)} copy(f32[16,128,128]{2,1,0:T(8,128)S(1)} %get-tuple-element.13) | data formatting | bytes 2097152
  (2 shorter events, 0.0 us)
Async XLA Ops:
  0.6 1.2 %copy-start = (f32[16,128,128]{2,1,0:T(8,128)S(1)}, f32[16,128,128]{2,1,0:T(8,128)}, u32[]{:S(2)}) copy-start(f32[16,128,128]{2,1,0:T(8,128)} %param.7) | copy-start | bytes 3145732
  0.6 1.2 %copy-start.2 = (bf16[128,4,128]{2,1,0:T(4,128)(2,1)S(1)}, bf16[128,4,128]{2,1,0:T(4,128)(2,1)}, u32[]{:S(2)}) copy-start(bf16[128,4,128]{2,1,0:T(4,128)(2,1)} %param.6) | copy-start | bytes 393220
  1.9 1.1 %copy-start.1 = (bf16[128,16,128]{2,1,0:T(8,128)(2,1)S(1)}, bf16[128,16,128]{2,1,0:T(8,128)(2,1)}, u32[]{:S(2)}) copy-start(bf16[128,16,128]{2,1,0:T(8,128)(2,1)} %param.4) | copy-start | bytes 1572868
where the time goes:
time: 70.8 us; the launch traced here: 70.7 us
  Pallas kernels  65.4 us (92%)
  local copies, waits for them, and re-layouts  4.52 us (6%)
    pallas_call x1, Pallas kernels, whole_head(): pl.pallas_call(head_kernel, out_shape=(jax.ShapeDtypeStruct((blocks, leng...  65.4 us
    unnamed x9, local copies, waits for them, and re-layouts  3.52 us

commit v1 on v0

--- a/solution.py
+++ b/solution.py
@@ -291,8 +291,7 @@
 def head_kernel(
     qt_ref, kvt_ref, w_ref, student_ref, update_ref,
     q_all, kv_all, mix_ref, gat_ref, gat_key_ref, sq_ref, own_ref, sum_ref, pre_ref, pre_norm_ref,
-    score_ref, kfeat_ref, gstate_ref, gnorm_ref, state_ref, norm_ref,
-    wq_ref, wk_ref, acc_ref, peak_ref, total_ref, gq_ref, gk_ref,
+    score_ref, near_ref, kfeat_ref, gstate_ref, gnorm_ref, wq_ref, wk_ref, gq_ref,
     q_send, q_recv, kv_send, kv_recv, kv_relay, local_sem, st_send, st_recv,
     g_send, g_relay, g_recv, sq_send, sq_recv,
 ):
@@ -303,7 +302,13 @@
     plane, spot = me // group, me % group
     features = w_ref.shape[1] // 2
     rows = 2 * length
-    steps = blocks // 2
+    steps, pairs = blocks // 2, blocks // 4
+    middle = pairs - 1
+    place = me // 2
+    my_pair = jnp.where(place % 2 == 0, place, steps - 1 - place) // 2
+
+    def pair_block(p, u):
+        return jnp.where(u < 2, 4 * p + u, blocks - 4 - 4 * p + u)
 
     gats = (gat_ref, gat_key_ref)
     barrier = pltpu.get_barrier_semaphore()
@@ -395,18 +400,19 @@
     own_q = pltpu.make_async_copy(qt_ref.at[me], q_all.at[me], local_sem.at[1])
     own_kv.start()
     own_q.start()
-    scale = 1.0 / math.sqrt(width)
+    rate = math.log2(math.e) / math.sqrt(width)
     lane = lax.broadcasted_iota(jnp.int32, (rows, 2 * features), 1)
     is_upper = lane < features
     row_half = lax.broadcasted_iota(jnp.int32, (2 * features, 2 * features), 0) < features
     col_half = lax.broadcasted_iota(jnp.int32, (2 * features, 2 * features), 1) < features
     halves = jnp.where(row_half == col_half, 1.0, 0.0).astype(bf16)
+    square = (rows, rows)
+    causal = lax.broadcasted_iota(jnp.int32, square, 1) <= lax.broadcasted_iota(jnp.int32, square, 0)
     w = w_ref[...]
     wq, wk = w[:, :features], w[:, features:]
     wq_ref[...] = cat(split(cat([wq, -wq], 1), 3), 0)
     wk_ref[...] = cat(split(cat([wk, -wk], 1), 3), 0)
-    for ref in (state_ref, norm_ref, gq_ref, gk_ref):
-        ref[...] = jnp.zeros_like(ref)
+    gq_ref[...] = jnp.zeros_like(gq_ref)
     own_kv.wait()
     own_q.wait()
 
@@ -450,21 +456,28 @@
 
         planes_but_mine(one)
 
-    def key_side(i):
-        kv_arrived(2 * i)
-        kv_arrived(2 * i + 1)
-        k, v = load(1, i), load(2, i)
-        kf = half_softmax(mxu(cat([k, k, k], 1), wk_ref[...], NN), is_upper, halves)
-        kfeat_ref[i] = kf
-        own_ref[2 * i] = wide_by_exact(kf[:length], v[:length], TN)
-        own_ref[2 * i + 1] = wide_by_exact(kf[length:], v[length:], TN)
-        sum_ref[2 * i] = jnp.sum(kf[:length], axis=0, keepdims=True)
-        sum_ref[2 * i + 1] = jnp.sum(kf[length:], axis=0, keepdims=True)
+    def key_side(pair):
+        each(4, lambda u: kv_arrived(4 * pair + u))
+        steps_of = (2 * pair, 2 * pair + 1)
+        ks, vs = ([load(part, i) for i in steps_of] for part in (1, 2))
+        kfs = [
+            half_softmax(mxu(cat([k, k, k], 1), wk_ref[...], NN), is_upper, halves) for k in ks
+        ]
+        for i, kf, v in zip(steps_of, kfs, vs):
+            kfeat_ref[i] = kf
+            for h in range(2):
+                part = kf[h * length:(h + 1) * length]
+                own_ref[2 * i + h] = wide_by_exact(part, v[h * length:(h + 1) * length], TN)
+                sum_ref[2 * i + h] = jnp.sum(part, axis=0, keepdims=True)
 
     def push(d):
-        q_copy((me + 2 * blocks - 1 - d) % blocks).start()
-
-    each(blocks - 1, push)
+        t = pair_block((my_pair + pairs - d // 4) % pairs, d % 4)
+
+        @pl.when(t != me)
+        def _():
+            q_copy(t).start()
+
+    each(blocks, push)
 
     def relay_first(dz):
         pass_on((plane + dz + 1) % planes)
@@ -472,8 +485,7 @@
     each(planes - 1, relay_first)
 
     def stage(dz):
-        half = group // 2
-        each(half, lambda u: key_side((plane + dz) % planes * half + u))
+        each(group // 4, lambda u: key_side((plane + dz) % planes * (group // 4) + u))
 
     each(planes, stage)
     for b in range(2):
@@ -487,136 +499,165 @@
     each(blocks - 2, prefix)
 
     def forward(turn, carry):
-        i = (me // 2 + turn) % steps
-        q_arrived(2 * i)
-        q_arrived(2 * i + 1)
-        q, v = load(0, i), load(2, i)
-        acc_ref[...] = jnp.zeros_like(acc_ref)
-        total_ref[...] = jnp.zeros_like(total_ref)
-        peak_ref[...] = jnp.full(peak_ref.shape, big_negative, f32)
+        p = (my_pair + turn) % pairs
+        a, b = 2 * p, steps - 1 - 2 * p
+        each(4, lambda u: q_arrived(pair_block(p, u)))
+        tokens = (a, b)
+        qs = [load(0, i) for i in tokens]
+        vs = [load(2, i) for i in tokens]
+        wide_b = b // 2
 
         def pair_of(part, j):
             return cat([load(part, 2 * j), load(part, 2 * j + 1)], 0)
 
-        def keep(j, s):
-            score_ref[2 * j] = s[:, :rows]
-            score_ref[2 * j + 1] = s[:, rows:]
-            top = jnp.maximum(s[:, :rows], s[:, rows:])
-            peak_ref[...] = jnp.maximum(
-                peak_ref[...], jnp.maximum(top[:, :length], top[:, length:])
-            )
-
-        last = i // 2
-        each(last, lambda j: keep(j, mxu(q, pair_of(1, j), NT) * scale))
-        s = mxu(q, pair_of(1, last), NT) * scale
-        column = lax.broadcasted_iota(jnp.int32, (rows, 2 * rows), 1)
-        row = lax.broadcasted_iota(jnp.int32, (rows, 2 * rows), 0)
-        keep(last, jnp.where(column <= row + (i - 2 * last) * rows, s, big_negative))
-        row_max = jnp.max(peak_ref[...], axis=-1, keepdims=True)
-
-        def weigh(j):
-            p0 = jnp.exp(score_ref[2 * j] - row_max)
-            p1 = jnp.exp(score_ref[2 * j + 1] - row_max)
-            both = p0 + p1
-            total_ref[...] += both[:, :length] + both[:, length:]
-            p = cat([p0.astype(bf16), p1.astype(bf16)], 1)
-            acc_ref[...] += mxu(p, pair_of(2, j), NN)
-
-        each(last + 1, weigh)
-        teacher = acc_ref[...] / jnp.sum(total_ref[...], axis=-1, keepdims=True)
-
-        before = jnp.maximum(i - 1, 0)
-        s = score_ref[i]
-        prev_top = score_ref[before, :length, length:]
-        prev_top = jnp.where(i > 0, prev_top, big_negative)
-        prev = cat([prev_top, s[length:, :length]], 0)
-        own = cat([s[:length, :length], s[length:, length:]], 0)
-        win_max = jnp.max(jnp.maximum(prev, own), axis=-1, keepdims=True)
-        p_prev, p_own = jnp.exp(prev - win_max), jnp.exp(own - win_max)
-        win_den = jnp.sum(p_prev + p_own, axis=-1, keepdims=True)
-        b_prev, b_own = p_prev.astype(bf16), p_own.astype(bf16)
-        v_before = kv_all[jnp.maximum(2 * i - 1, 0), 1]
-        win_num = cat(
-            [
-                mxu(cat([b_prev[:length], b_own[:length]], 1), cat([v_before, v[:length]], 0), NN),
-                mxu(cat([b_prev[length:], b_own[length:]], 1), v, NN),
-            ],
-            0,
-        )
-
-        qf = half_softmax(mxu(cat([q, q, q], 1), wq_ref[...], NN), is_upper, halves)
-        state_0, norm_0 = pre_ref[2 * i], pre_norm_ref[2 * i]
-        state_1, norm_1 = pre_ref[2 * i + 1], pre_norm_ref[2 * i + 1]
-
-        norm = cat(
-            [
-                jnp.broadcast_to(norm_0, (length, 2 * features)),
-                jnp.broadcast_to(norm_1, (length, 2 * features)),
-            ],
-            0,
-        )
-        decay = jnp.exp(-win_max)
-        far = cat(
-            [wide_by_wide(qf[:length], state_0, NN), wide_by_wide(qf[length:], state_1, NN)], 0
-        )
-        den = win_den + decay * jnp.sum(qf * norm, axis=-1, keepdims=True)
-        mix = (win_num + decay * far) / den
-        mix_ref[pl.ds(2 * i, 2)] = mix.astype(bf16).reshape(2, length, width)
-        send_student(2 * i)
-        send_student(2 * i + 1)
-        mismatch = mix - teacher
-        g_num = mismatch / den
-        g_den = -jnp.sum(mismatch * mix, axis=-1, keepdims=True) / den
-        lifted = decay * qf
-        gstate_ref[2 * i] = wide_by_wide(lifted[:length], g_num[:length], TN)
-        gstate_ref[2 * i + 1] = wide_by_wide(lifted[length:], g_num[length:], TN)
-        pulled_norm = lifted * g_den
-        gnorm_ref[2 * i] = jnp.sum(pulled_norm[:length], axis=0, keepdims=True)
-        gnorm_ref[2 * i + 1] = jnp.sum(pulled_norm[length:], axis=0, keepdims=True)
-        g_qf = decay * (
+        def fold(x, combine):
+            while x.shape[1] > length:
+                half = x.shape[1] // 2
+                x = combine(x[:, :half], x[:, half:])
+            return x
+
+        s = mxu(qs[0], load(1, a), NT) * rate
+        s_a = jnp.where(causal, s, big_negative)
+        near_ref[0] = s_a
+        s = mxu(qs[1], pair_of(1, wide_b), NT) * rate
+        s_b = [s[:, :rows], jnp.where(causal, s[:, rows:], big_negative)]
+        near_ref[1], near_ref[2] = s_b
+        peaks = [fold(s_a, jnp.maximum), fold(jnp.maximum(*s_b), jnp.maximum)]
+
+        def far_tile(m):
+            first = m < p
+            return first, jnp.where(first, a, b), jnp.where(first, m, m - p)
+
+        for m in range(middle):
+            first, i, j = far_tile(m)
+            s = mxu(load(0, i), pair_of(1, j), NT) * rate
+            score_ref[m] = s
+            top = fold(s, jnp.maximum)
+            peaks = [
+                jnp.maximum(peaks[0], jnp.where(first, top, big_negative)),
+                jnp.maximum(peaks[1], jnp.where(first, big_negative, top)),
+            ]
+        tops = [jnp.max(x, axis=-1, keepdims=True) for x in peaks]
+
+        weight = jnp.exp2(near_ref[0] - tops[0])
+        sums = [fold(weight, jnp.add)]
+        accs = [mxu(weight.astype(bf16), vs[0], NN)]
+        weight = jnp.exp2(cat([near_ref[1], near_ref[2]], 1) - tops[1])
+        sums.append(fold(weight, jnp.add))
+        accs.append(mxu(weight.astype(bf16), pair_of(2, wide_b), NN))
+        for m in range(middle):
+            first, i, j = far_tile(m)
+            weight = jnp.exp2(score_ref[m] - jnp.where(first, tops[0], tops[1]))
+            part = fold(weight, jnp.add)
+            prod = mxu(weight.astype(bf16), pair_of(2, j), NN)
+            sums = [sums[0] + jnp.where(first, part, 0.0), sums[1] + jnp.where(first, 0.0, part)]
+            accs = [accs[0] + jnp.where(first, prod, 0.0), accs[1] + jnp.where(first, 0.0, prod)]
+        teachers = [
+            acc / jnp.sum(total, axis=-1, keepdims=True) for acc, total in zip(accs, sums)
+        ]
+
+        def halves_of(f):
+            return [cat([f(x, 0), f(x, 1)], 0) for x in range(2)]
+
+        def cut(x, half):
+            return x[half * length:(half + 1) * length]
+
+        last_far = score_ref[jnp.maximum(p - 1, 0), :length, 3 * length:]
+        prevs = [
+            cat([jnp.where(p > 0, last_far, big_negative), near_ref[0, length:, :length]], 0),
+            cat([near_ref[1, :length, length:], near_ref[2, length:, :length]], 0),
+        ]
+        owns = [
+            cat([near_ref[k, :length, :length], near_ref[k, length:, length:]], 0) for k in (0, 2)
+        ]
+        win_maxs = [
+            jnp.max(jnp.maximum(prev, own), axis=-1, keepdims=True)
+            for prev, own in zip(prevs, owns)
+        ]
+        p_prevs = [jnp.exp2(x - top) for x, top in zip(prevs, win_maxs)]
+        p_owns = [jnp.exp2(x - top) for x, top in zip(owns, win_maxs)]
+        win_dens = [jnp.sum(x + y, axis=-1, keepdims=True) for x, y in zip(p_prevs, p_owns)]
+        p_wins = [cat([x.astype(bf16), y.astype(bf16)], 1) for x, y in zip(p_prevs, p_owns)]
+        v_befores = [kv_all[jnp.maximum(2 * i - 1, 0), 1] for i in tokens]
+        v_wins = [
+            (cat([before, v[:length]], 0), v) for before, v in zip(v_befores, vs)
+        ]
+        win_nums = halves_of(lambda x, h: mxu(cut(p_wins[x], h), v_wins[x][h], NN))
+
+        qfs = [
+            half_softmax(mxu(cat([q, q, q], 1), wq_ref[...], NN), is_upper, halves) for q in qs
+        ]
+        states = [[pre_ref[2 * i], pre_ref[2 * i + 1]] for i in tokens]
+        norms = [
             cat(
                 [
-                    wide_by_wide(g_num[:length], state_0, NT),
-                    wide_by_wide(g_num[length:], state_1, NT),
+                    jnp.broadcast_to(pre_norm_ref[2 * i + h], (length, 2 * features))
+                    for h in range(2)
                 ],
                 0,
             )
-            + norm * g_den
-        )
-        d_q = qf * (g_qf - half_sum(qf * g_qf, halves))
-        gq_ref[...] += wide_by_exact(d_q, q, TN)
+            for i in tokens
+        ]
+        decays = [jnp.exp2(-top) for top in win_maxs]
+        fars = halves_of(lambda x, h: wide_by_wide(cut(qfs[x], h), states[x][h], NN))
+        dens = [
+            win_den + decay * jnp.sum(qf * norm, axis=-1, keepdims=True)
+            for win_den, decay, qf, norm in zip(win_dens, decays, qfs, norms)
+        ]
+        mixes = [
+            (num + decay * far) / den
+            for num, decay, far, den in zip(win_nums, decays, fars, dens)
+        ]
+        for i, mix in zip(tokens, mixes):
+            mix_ref[pl.ds(2 * i, 2)] = mix.astype(bf16).reshape(2, length, width)
+        each(4, lambda u: send_student(pair_block(p, u)))
+        mismatches = [mix - teacher for mix, teacher in zip(mixes, teachers)]
+        g_nums = [x / den for x, den in zip(mismatches, dens)]
+        g_dens = [
+            -jnp.sum(x * mix, axis=-1, keepdims=True) / den
+            for x, mix, den in zip(mismatches, mixes, dens)
+        ]
+        lifts = [decay * qf for decay, qf in zip(decays, qfs)]
+        pulled_norms = [lift * g_den for lift, g_den in zip(lifts, g_dens)]
+        for x, i in enumerate(tokens):
+            for h in range(2):
+                gstate_ref[2 * i + h] = wide_by_wide(cut(lifts[x], h), cut(g_nums[x], h), TN)
+                gnorm_ref[2 * i + h] = jnp.sum(cut(pulled_norms[x], h), axis=0, keepdims=True)
+        pulled = halves_of(lambda x, h: wide_by_wide(cut(g_nums[x], h), states[x][h], NT))
+        g_qfs = [
+            decay * (pull + norm * g_den)
+            for decay, pull, norm, g_den in zip(decays, pulled, norms, g_dens)
+        ]
+        d_qs = [qf * (g - half_sum(qf * g, halves)) for qf, g in zip(qfs, g_qfs)]
+        gq_ref[...] += wide_by_exact(d_qs[0], qs[0], TN) + wide_by_exact(d_qs[1], qs[1], TN)
         return carry
 
-    lax.fori_loop(0, steps, forward, 0)
+    lax.fori_loop(0, pairs, forward, 0)
     gat_ref[me] = (gq_ref[:features] - gq_ref[features:]).astype(bf16)
     send_grad(0)
 
-    for ref in (state_ref, norm_ref):
-        ref[...] = jnp.zeros_like(ref)
-
-    def backward(step, carry):
-        i = steps - 1 - step
-        k, v, kf = load(1, i), load(2, i), kfeat_ref[i]
-        nxt = jnp.minimum(i + 1, steps - 1)
-        live = jnp.where(step > 0, 1.0, 0.0)
-        later_1, later_n1 = state_ref[...], norm_ref[...]
-        later_0 = later_1 + live * gstate_ref[2 * nxt]
-        later_n0 = later_n1 + live * gnorm_ref[2 * nxt]
-        g_kf = cat(
-            [
-                exact_by_wide(v[:length], later_0, NT) + later_n0,
-                exact_by_wide(v[length:], later_1, NT) + later_n1,
-            ],
-            0,
-        )
-        d_k = kf * (g_kf - half_sum(kf * g_kf, halves))
-        gk_ref[...] += wide_by_exact(d_k, k, TN)
-        state_ref[...] = later_0 + gstate_ref[2 * i + 1]
-        norm_ref[...] = later_n0 + gnorm_ref[2 * i + 1]
-        return carry
-
-    lax.fori_loop(0, steps, backward, 0)
-    gat_key_ref[me] = (gk_ref[:features] - gk_ref[features:]).astype(bf16)
+    for b in range(blocks - 2, 1, -1):
+        gstate_ref[b] = gstate_ref[b] + gstate_ref[b + 1]
+        gnorm_ref[b] = gnorm_ref[b] + gnorm_ref[b + 1]
+
+    def backward(group_of):
+        ks, vs, kfs = ([f(i) for i in group_of] for f in (lambda i: load(1, i), lambda i: load(2, i), lambda i: kfeat_ref[i]))
+        g_kfs = [
+            cat(
+                [
+                    exact_by_wide(v[h * length:(h + 1) * length], gstate_ref[2 * i + h + 2], NT)
+                    + gnorm_ref[2 * i + h + 2]
+                    for h in range(2)
+                ],
+                0,
+            )
+            for i, v in zip(group_of, vs)
+        ]
+        d_ks = [kf * (g - half_sum(kf * g, halves)) for kf, g in zip(kfs, g_kfs)]
+        return [wide_by_exact(d_k, k, TN) for d_k, k in zip(d_ks, ks)]
+
+    gk = sum(backward(range(steps // 2)) + backward(range(steps // 2, steps - 1)))
+    gat_key_ref[me] = (gk[:features] - gk[features:]).astype(bf16)
     send_grad(1)
     relay_grad(0)
     relay_grad(1)
@@ -637,10 +678,9 @@
     swap = remote(sq_ref.at[0], sq_ref.at[1], sq_send.at[0], sq_recv.at[0], head=1 - side)
     swap.start()
 
-    def turned(b):
+    for b in range(blocks):
         update_ref[b] = cat([gat_ref[b], gat_key_ref[b]], 0).astype(f32).T
 
-    each(blocks, turned)
 
     def settle(t):
         @pl.when(t != me)
@@ -671,10 +711,8 @@
     total = jnp.sum(sq_ref[0] + sq_ref[1], keepdims=True)
     inverse = 1.0 / jnp.sqrt(total / entries + 1e-06)
 
-    def scaled(b):
+    for b in range(blocks):
         update_ref[b] = update_ref[b] * inverse
-
-    each(blocks, scaled)
 
 
 def whole_head(qt, kvt, w):
@@ -703,18 +741,13 @@
             vmem((blocks, 1, double), f32),
             vmem((blocks, double, width), f32),
             vmem((blocks, 1, double), f32),
-            vmem((steps, rows, rows), f32),
+            vmem((blocks // 4 - 1, rows, 2 * rows), f32),
+            vmem((3, rows, rows), f32),
             vmem((steps, rows, double), f32),
             vmem((blocks, double, width), f32),
             vmem((blocks, 1, double), f32),
-            vmem((double, width), f32),
-            vmem((1, double), f32),
             vmem((3 * width, double), bf16),
             vmem((3 * width, double), bf16),
-            vmem((rows, width), f32),
-            vmem((rows, length), f32),
-            vmem((rows, length), f32),
-            vmem((double, width), f32),
             vmem((double, width), f32),
             dma((blocks,)),
             dma((blocks,)),
@@ -748,7 +781,7 @@
     count = lax.axis_size("ctx")
     width = queries.shape[2]
     fits = queries.shape[1] == count and lax.axis_size("head") == 2 and count % 4 == 0 and count * queries.shape[0] <= 4096
-    fits = fits and queries.shape[1] // keys.shape[1] % 2 == 0 and queries.shape[0] == width and feature_weight.shape[2] == width
+    fits = fits and queries.shape[1] // keys.shape[1] % 4 == 0 and queries.shape[0] == width and feature_weight.shape[2] == width
     body = head_shards if fits else general_shards
     return body(queries, keys, values, feature_weight)
 

time: 70.8 us -> 59.6 us (0.84)
  Pallas kernels: 65.4 us -> 54.2 us
    pallas_call x1, Pallas kernels: 65.4 us -> 54.2 us  [whole_head(): pl.pallas_call(head_kernel, out_shape=(jax.ShapeDtypeStruct((blocks, leng...]
where the time goes in v1:
time: 59.6 us; the launch traced here: 59.4 us
  Pallas kernels  54.2 us (91%)
  local copies, waits for them, and re-layouts  4.52 us (8%)
  between operations  0.68 us (1%)
    pallas_call x1, Pallas kernels, whole_head(): pl.pallas_call(head_kernel, out_shape=(jax.ShapeDtypeStruct((blocks, leng...  54.2 us
    unnamed x9, local copies, waits for them, and re-layouts  3.52 us

profile of v1, /device:TPU:0, one launch (start us, length us, event | category | flops | bytes accessed | tf_op | source)
XLA Modules:
  0.0 59.4 jit_solution(9559039199846231662)
XLA Ops:
  0.6 0.0 copy-start
  0.6 0.0 copy-start.2
  0.7 1.2 %copy-done = f32[16,128,128]{2,1,0:T(8,128)S(1)} copy-done((f32[16,128,128]{2,1,0:T(8,128)S(1)}, f32[16,128,128]{2,1,0:T(8,128)}, u32[]{:S(2)}) %copy-start) | copy-done | bytes 1048600
  1.9 0.0 copy-done.2
  1.9 0.0 copy-start.1
  1.9 1.0 %copy_bitcast_fusion.1 = (bf16[1,128,4,128]{3,1,0,2:T(8,128)(2,1)S(1)}, bf16[1,128,4,128]{3,1,0,2:T(8,128)(2,1)S(1)}) fusion(bf16[128,4,128]{2,1,0:T(4,128)(2,1)S(1)} %copy-done.2, bf16[128,4,128]{2,1,0:T(4,128)(2,1)} %param.5), kind=kLoop, calls=%fused_computation.2 | loop fusion | bytes 524288 | tf_op jit(solution)/shard_map/stack | solution.py:774
  2.9 0.1 copy-done.1
  3.0 0.1 copy.13
  3.1 54.2 %shard_map.59 = (bf16[16,128,128]{2,1,0:T(8,128)(2,1)S(1)}, f32[16,128,128]{2,1,0:T(8,128)S(1)}) custom-call(bf16[16,128,128]{2,1,0:T(8,128)(2,1)S(1)} %bitcast.12, bf16[4,2,128,128]{3,2,1,0:T(8,128)(2,1)S(1)} %maximum_bitcast_fusion.kvt_ref, f32[128,128]{1,0:T(8,128)S(1)} %dynamic-slice_bitcast_fusion.w_ref), custom_call_target="tpu_custom_call" | custom-call | tf_op jit(solution)/shard_map/pallas_call | solution.py:725
  57.3 1.1 %copy.9 = bf16[128,16,128]{2,1,0:T(8,128)(2,1)} copy(bf16[128,16,128]{2,0,1:T(8,128)(2,1)S(1)} %bitcast.13) | data formatting | bytes 1048576
  58.4 1.0 %copy.15 = f32[16,128,128]{2,1,0:T(8,128)} copy(f32[16,128,128]{2,1,0:T(8,128)S(1)} %get-tuple-element.13) | data formatting | bytes 2097152
  (2 shorter events, 0.0 us)
Async XLA Ops:
  0.6 1.2 %copy-start = (f32[16,128,128]{2,1,0:T(8,128)S(1)}, f32[16,128,128]{2,1,0:T(8,128)}, u32[]{:S(2)}) copy-start(f32[16,128,128]{2,1,0:T(8,128)} %param.7) | copy-start | bytes 3145732
  0.6 1.2 %copy-start.2 = (bf16[128,4,128]{2,1,0:T(4,128)(2,1)S(1)}, bf16[128,4,128]{2,1,0:T(4,128)(2,1)}, u32[]{:S(2)}) copy-start(bf16[128,4,128]{2,1,0:T(4,128)(2,1)} %param.6) | copy-start | bytes 393220
  1.9 1.1 %copy-start.1 = (bf16[128,16,128]{2,1,0:T(8,128)(2,1)S(1)}, bf16[128,16,128]{2,1,0:T(8,128)(2,1)}, u32[]{:S(2)}) copy-start(bf16[128,16,128]{2,1,0:T(8,128)(2,1)} %param.4) | copy-start | bytes 1572868

commit v2 on v1

--- a/solution.py
+++ b/solution.py
@@ -289,117 +289,135 @@
 
 
 def head_kernel(
-    qt_ref, kvt_ref, w_ref, student_ref, update_ref,
-    q_all, kv_all, mix_ref, gat_ref, gat_key_ref, sq_ref, own_ref, sum_ref, pre_ref, pre_norm_ref,
+    q_hbm, k_hbm, v_hbm, w_hbm, student_hbm, grad_hbm, scale_hbm,
+    q_raw, k_raw, v_raw, w_ref, qt_ref, kvt_ref, q_all, kv_all, st_all, st_turned, mix_ref,
+    own_grad, gat_ref, sq_ref, scale_ref, own_ref, sum_ref, pre_ref, pre_norm_ref,
     score_ref, near_ref, kfeat_ref, gstate_ref, gnorm_ref, wq_ref, wk_ref, gq_ref,
-    q_send, q_recv, kv_send, kv_recv, kv_relay, local_sem, st_send, st_recv,
-    g_send, g_relay, g_recv, sq_send, sq_recv,
+    q_send, q_recv, kv_send, kv_recv, kv_cross, kv_sibling, local_sem, st_send, st_recv,
+    g_send, g_relay, g_recv, sq_send, sq_recv, fetch_sem, w_send, w_recv, out_sem,
 ):
     blocks, length, width = qt_ref.shape
     planes = kvt_ref.shape[0]
     group = blocks // planes
     me, side = lax.axis_index("ctx"), lax.axis_index("head")
     plane, spot = me // group, me % group
+    row, column = spot // 2, spot % 2
+    native = row == side
+    mine = plane * group + 2 * column + side
     features = w_ref.shape[1] // 2
     rows = 2 * length
     steps, pairs = blocks // 2, blocks // 4
     middle = pairs - 1
-    place = me // 2
-    my_pair = jnp.where(place % 2 == 0, place, steps - 1 - place) // 2
 
     def pair_block(p, u):
         return jnp.where(u < 2, 4 * p + u, blocks - 4 - 4 * p + u)
 
-    gats = (gat_ref, gat_key_ref)
+    my_pair = jnp.where(row == 0, plane, planes - 1 - plane)
     barrier = pltpu.get_barrier_semaphore()
 
-    def greet(t):
-        @pl.when(t != me)
+    def greet(t, h):
+        pl.semaphore_signal(
+            barrier, inc=1, device_id={"ctx": t, "head": h}, device_id_type=pl.DeviceIdType.MESH
+        )
+
+    def greet_side(d):
+        t = (me + d) % blocks
+
+        @pl.when(jnp.logical_not(native & (t == me)))
         def _():
-            pl.semaphore_signal(
-                barrier, inc=1, device_id={"ctx": t}, device_id_type=pl.DeviceIdType.MESH
-            )
-
-    each(blocks, greet)
-    pl.semaphore_signal(
-        barrier, inc=1, device_id={"head": 1 - side}, device_id_type=pl.DeviceIdType.MESH
-    )
-    pl.semaphore_wait(barrier, blocks)
-
-    def kv_column(g):
+            greet(t, row)
+
+    each(blocks, greet_side)
+    each(blocks // 2, lambda n: greet((n // 2) * group + 2 * side + n % 2, 1 - row))
+    fetches = [
+        pltpu.make_async_copy(src, dst, fetch_sem.at[n])
+        for n, (src, dst) in enumerate([(k_hbm, k_raw), (v_hbm, v_raw), (q_hbm, q_raw)])
+    ]
+    for fetch in fetches:
+        fetch.start()
+    own_w = pltpu.make_async_copy(w_hbm.at[mine], w_ref, local_sem.at[2])
+
+    @pl.when(native)
+    def _():
+        own_w.start()
+
+    def flip(index, d):
+        bit = 1
+        while bit <= d:
+            if d & bit:
+                index = index + bit - 2 * bit * ((index // bit) % 2)
+            bit *= 2
+        return index
+
+    def w_copy():
+        other = plane * group + 2 * column + 1 - side
+        return remote(w_hbm.at[other], w_ref, w_send.at[0], w_recv.at[0], ctx=me, head=1 - side)
+
+    def kv_land(g):
         return remote(
-            kvt_ref.at[g], kv_all.at[me], kv_send.at[g], kv_recv.at[me], ctx=g * group + spot
-        )
-
-    def kv_own(r):
+            kvt_ref.at[g], kv_all.at[me], kv_send.at[g], kv_recv.at[me],
+            ctx=g * group + 2 * side + column, head=row,
+        )
+
+    def landed_block(z):
+        return z * group + 2 * side + column
+
+    def crossed_block(z):
+        return z * group + 2 * side + 1 - column
+
+    def kv_across(z):
+        block = landed_block(z)
         return remote(
-            kvt_ref.at[plane], kv_all.at[me], kv_relay.at[plane, r], kv_recv.at[me],
-            ctx=plane * group + r,
-        )
-
-    def kv_pass(z, r):
-        block = z * group + spot
+            kv_all.at[block], kv_all.at[block], kv_cross.at[z], kv_recv.at[block],
+            ctx=plane * group + 2 * row + 1 - column, head=side,
+        )
+
+    def kv_share(block, n):
         return remote(
-            kv_all.at[block], kv_all.at[block], kv_relay.at[z, r], kv_recv.at[block],
-            ctx=plane * group + r,
-        )
-
-    def q_copy(t):
-        return remote(qt_ref.at[t], q_all.at[me], q_send.at[t], q_recv.at[me], ctx=t)
+            kv_all.at[block], kv_all.at[block], kv_sibling.at[n], kv_recv.at[block],
+            ctx=me, head=1 - side,
+        )
+
+    def q_copy(j):
+        return remote(
+            qt_ref.at[j], q_all.at[me], q_send.at[j], q_recv.at[me],
+            ctx=(j // group) * group + 2 * side + (j % group) // 2, head=j % 2,
+        )
 
     def q_arrival(b):
-        return remote(qt_ref.at[b], q_all.at[b], q_send.at[b], q_recv.at[b], ctx=b)
+        return remote(qt_ref.at[b], q_all.at[b], q_send.at[b], q_recv.at[b], ctx=b, head=row)
 
     def kv_arrival(b):
+        return remote(kv_all.at[b], kv_all.at[b], kv_send.at[0], kv_recv.at[b], ctx=b, head=row)
+
+    def st_copy(b):
+        return remote(mix_ref.at[b], st_all.at[mine], st_send.at[b], st_recv.at[mine], ctx=b, head=row)
+
+    def st_arrival(j):
+        return remote(mix_ref.at[j], st_all.at[j], st_send.at[j], st_recv.at[j], ctx=j, head=row)
+
+    def g_column(part, z):
         return remote(
-            kv_all.at[b], kv_all.at[b], kv_send.at[0], kv_recv.at[b], ctx=b
-        )
-
-    def st_copy(b):
-        return remote(mix_ref.at[b], student_ref.at[me], st_send.at[b], st_recv.at[me], ctx=b)
-
-    def st_arrival(b):
-        return remote(mix_ref.at[b], student_ref.at[b], st_send.at[b], st_recv.at[b], ctx=b)
-
-    def g_column(part, z):
-        piece = gats[part].at[me]
+            own_grad.at[part], gat_ref.at[part, mine], g_send.at[part, z], g_recv.at[part, mine],
+            ctx=z * group + spot, head=row,
+        )
+
+    def g_pass(part, j, d):
+        piece = gat_ref.at[part, j]
         return remote(
-            piece, piece, g_send.at[part, z], g_recv.at[me, part], ctx=z * group + spot
-        )
-
-    def g_pass(part, z, r):
-        block = z * group + spot
-        piece = gats[part].at[block]
-        return remote(
-            piece, piece, g_relay.at[part, z, r], g_recv.at[block, part], ctx=plane * group + r
-        )
-
-    def g_arrival(part, b):
-        piece = gats[part].at[b]
-        return remote(piece, piece, g_send.at[part, 0], g_recv.at[b, part], ctx=b)
-
-    def planes_but_mine(body):
-        def one(z):
-            @pl.when(z != plane)
-            def _():
-                body(z)
-
-        each(planes, one)
-
-    def spots_but_mine(body):
-        def one(r):
-            @pl.when(r != spot)
-            def _():
-                body(r)
-
-        each(group, one)
-
-    planes_but_mine(lambda g: kv_column(g).start())
-    spots_but_mine(lambda r: kv_own(r).start())
-    own_kv = pltpu.make_async_copy(kvt_ref.at[plane], kv_all.at[me], local_sem.at[0])
-    own_q = pltpu.make_async_copy(qt_ref.at[me], q_all.at[me], local_sem.at[1])
-    own_kv.start()
-    own_q.start()
+            piece, piece, g_relay.at[part, j, d - 1], g_recv.at[part, j],
+            ctx=plane * group + flip(spot, d), head=side,
+        )
+
+    def g_arrival(part, j):
+        piece = gat_ref.at[part, j]
+        return remote(piece, piece, g_send.at[part, 0], g_recv.at[part, j], ctx=j, head=row)
+
+    def unless_own(b, body):
+        @pl.when(jnp.logical_not(native & (b == me)))
+        def _():
+            body()
+
     rate = math.log2(math.e) / math.sqrt(width)
     lane = lax.broadcasted_iota(jnp.int32, (rows, 2 * features), 1)
     is_upper = lane < features
@@ -408,18 +426,50 @@
     halves = jnp.where(row_half == col_half, 1.0, 0.0).astype(bf16)
     square = (rows, rows)
     causal = lax.broadcasted_iota(jnp.int32, square, 1) <= lax.broadcasted_iota(jnp.int32, square, 0)
-    w = w_ref[...]
-    wq, wk = w[:, :features], w[:, features:]
-    wq_ref[...] = cat(split(cat([wq, -wq], 1), 3), 0)
-    wk_ref[...] = cat(split(cat([wk, -wk], 1), 3), 0)
-    gq_ref[...] = jnp.zeros_like(gq_ref)
-    own_kv.wait()
-    own_q.wait()
-
-    def pass_on(z):
-        kv_arrival(z * group + spot).wait_recv()
-        spots_but_mine(lambda r: kv_pass(z, r).start())
-
+    for part, (fetch, raw) in enumerate(zip(fetches, (k_raw, v_raw))):
+        fetch.wait()
+        kvt_ref[:, part] = jnp.transpose(raw[...], (1, 0, 2))
+    own_kv = pltpu.make_async_copy(kvt_ref.at[plane], kv_all.at[me], local_sem.at[0])
+
+    @pl.when(native)
+    def _():
+        own_kv.start()
+
+    pl.semaphore_wait(barrier, jnp.where(native, 3 * blocks // 2 - 1, 3 * blocks // 2))
+    for d in range(planes):
+        g = flip(plane, d)
+        if d == 0:
+            @pl.when(jnp.logical_not(native))
+            def _():
+                kv_land(g).start()
+        else:
+            kv_land(g).start()
+
+    @pl.when(native)
+    def _():
+        w_copy().start()
+
+    fetches[2].wait()
+    qt_ref[...] = jnp.transpose(q_raw[...], (1, 0, 2))
+    own_q = pltpu.make_async_copy(qt_ref.at[mine], q_all.at[me], local_sem.at[1])
+
+    @pl.when(native)
+    def _():
+        own_q.start()
+        own_kv.wait()
+
+    def land(d):
+        z = flip(plane, d)
+        block = landed_block(z)
+        unless_own(block, lambda: kv_arrival(block).wait_recv())
+        kv_across(z).start()
+        kv_share(block, z).start()
+
+    def cross(d):
+        z = flip(plane, d)
+        block = crossed_block(z)
+        kv_arrival(block).wait_recv()
+        kv_share(block, planes + z).start()
 
     def load(part, i):
         if part == 0:
@@ -427,34 +477,47 @@
         return kv_all[pl.ds(2 * i, 2), part - 1].reshape(rows, width)
 
     def q_arrived(b):
-        @pl.when(b != me)
-        def _():
-            q_arrival(b).wait_recv()
+        unless_own(b, lambda: q_arrival(b).wait_recv())
 
     def kv_arrived(b):
-        @pl.when(b % group != spot)
+        @pl.when((b % group) // 2 != side)
         def _():
             kv_arrival(b).wait_recv()
 
     def send_student(b):
-        @pl.when(b != me)
+        unless_own(b, lambda: st_copy(b).start())
+
+        @pl.when(native & (b == me))
         def _():
-            st_copy(b).start()
-
-        @pl.when(b == me)
+            st_all[mine] = mix_ref[me]
+
+    def send_grad(part):
+        for d in range(planes):
+            z = flip(plane, d)
+            if d == 0:
+                @pl.when(native)
+                def _():
+                    gat_ref[part, mine] = own_grad[part]
+
+                @pl.when(jnp.logical_not(native))
+                def _():
+                    g_column(part, z).start()
+            else:
+                g_column(part, z).start()
+
+    def relay_grad(part):
+        @pl.when(native)
         def _():
-            student_ref[me] = mix_ref[me]
-
-    def send_grad(part):
-        planes_but_mine(lambda z: g_column(part, z).start())
-        spots_but_mine(lambda r: g_pass(part, plane, r).start())
-
-    def relay_grad(part):
-        def one(z):
-            g_arrival(part, z * group + spot).wait_recv()
-            spots_but_mine(lambda r: g_pass(part, z, r).start())
-
-        planes_but_mine(one)
+            for z in range(planes):
+                for h in range(2):
+                    j = flip(plane, z) * group + 2 * column + h
+
+                    @pl.when(j != mine)
+                    def _():
+                        g_arrival(part, j).wait_recv()
+
+                    for d in range(1, group):
+                        g_pass(part, j, d).start()
 
     def key_side(pair):
         each(4, lambda u: kv_arrived(4 * pair + u))
@@ -470,24 +533,51 @@
                 own_ref[2 * i + h] = wide_by_exact(part, v[h * length:(h + 1) * length], TN)
                 sum_ref[2 * i + h] = jnp.sum(part, axis=0, keepdims=True)
 
-    def push(d):
-        t = pair_block((my_pair + pairs - d // 4) % pairs, d % 4)
-
-        @pl.when(t != me)
+    def push(n):
+        p = (my_pair + pairs - n // group) % pairs
+        j = jnp.where(side == 0, p, planes - 1 - p) * group + n % group
+
+        @pl.when(jnp.logical_not(native & (j == mine)))
         def _():
-            q_copy(t).start()
-
-    each(blocks, push)
-
-    def relay_first(dz):
-        pass_on((plane + dz + 1) % planes)
-
-    each(planes - 1, relay_first)
-
-    def stage(dz):
-        each(group // 4, lambda u: key_side((plane + dz) % planes * (group // 4) + u))
-
-    each(planes, stage)
+            q_copy(j).start()
+
+    def plane_keys(z):
+        each(group // 4, lambda u: key_side(z * (group // 4) + u))
+
+    def push_turns(first, last):
+        each((last - first) * group, lambda n: push(first * group + n))
+
+    land(0)
+    land(1)
+    cross(0)
+    push_turns(0, 1)
+    land(2)
+    cross(1)
+    land(3)
+    cross(2)
+    cross(3)
+
+    @pl.when(native)
+    def _():
+        own_w.wait()
+
+    @pl.when(jnp.logical_not(native))
+    def _():
+        w_copy().wait_recv()
+
+    w = w_ref[...]
+    wq, wk = w[:, :features], w[:, features:]
+    wq_ref[...] = cat(split(cat([wq, -wq], 1), 3), 0)
+    wk_ref[...] = cat(split(cat([wk, -wk], 1), 3), 0)
+    gq_ref[...] = jnp.zeros_like(gq_ref)
+    push_turns(1, pairs)
+    for d in range(planes):
+        plane_keys(flip(plane, d))
+
+    @pl.when(native)
+    def _():
+        own_q.wait()
+
     for b in range(2):
         pre_ref[b] = jnp.zeros_like(pre_ref[b])
         pre_norm_ref[b] = jnp.zeros_like(pre_norm_ref[b])
@@ -633,7 +723,7 @@
         return carry
 
     lax.fori_loop(0, pairs, forward, 0)
-    gat_ref[me] = (gq_ref[:features] - gq_ref[features:]).astype(bf16)
+    own_grad[0] = (gq_ref[:features] - gq_ref[features:]).astype(bf16)
     send_grad(0)
 
     for b in range(blocks - 2, 1, -1):
@@ -657,86 +747,162 @@
         return [wide_by_exact(d_k, k, TN) for d_k, k in zip(d_ks, ks)]
 
     gk = sum(backward(range(steps // 2)) + backward(range(steps // 2, steps - 1)))
-    gat_key_ref[me] = (gk[:features] - gk[features:]).astype(bf16)
+    own_grad[1] = (gk[:features] - gk[features:]).astype(bf16)
     send_grad(1)
     relay_grad(0)
     relay_grad(1)
 
-    def gathered(b):
-        @pl.when(b % group != spot)
+    def unless_mine(j, body):
+        @pl.when(jnp.logical_not(native & (j == mine)))
         def _():
-            g_arrival(0, b).wait_recv()
-            g_arrival(1, b).wait_recv()
+            body()
+
+    each(blocks, lambda j: unless_mine(j, lambda: st_arrival(j).wait_recv()))
+    st_turned[...] = jnp.transpose(st_all[...], (1, 0, 2))
+    student_out = pltpu.make_async_copy(st_turned, student_hbm, out_sem.at[0])
+    student_out.start()
+
+    def gathered(j):
+        relayed = native & ((j % group) // 2 == column)
+
+        @pl.when(jnp.logical_not(relayed))
+        def _():
+            g_arrival(0, j).wait_recv()
+            g_arrival(1, j).wait_recv()
 
     each(blocks, gathered)
+    grad_out = pltpu.make_async_copy(gat_ref, grad_hbm, out_sem.at[1])
+    grad_out.start()
     squares = jnp.zeros((8, width), f32)
-    for b in range(blocks):
-        piece = cat([gat_ref[b], gat_key_ref[b]], 0).astype(f32)
+    for j in range(blocks):
+        piece = cat([gat_ref[0, j], gat_ref[1, j]], 0).astype(f32)
         piece = piece.reshape(2 * features // 8, 8, width)
         squares = squares + jnp.sum(piece * piece, axis=0)
     sq_ref[0] = squares
-    swap = remote(sq_ref.at[0], sq_ref.at[1], sq_send.at[0], sq_recv.at[0], head=1 - side)
+    swap = remote(
+        sq_ref.at[0], sq_ref.at[1], sq_send.at[0], sq_recv.at[0], ctx=me, head=1 - side
+    )
     swap.start()
 
-    for b in range(blocks):
-        update_ref[b] = cat([gat_ref[b], gat_key_ref[b]], 0).astype(f32).T
-
-
-    def settle(t):
-        @pl.when(t != me)
+    def settle(j):
+        unless_mine(j, lambda: q_copy(j).wait_send())
+        unless_own(j, lambda: st_copy(j).wait_send())
+
+    each(blocks, settle)
+
+    def settle_plane(z):
+        @pl.when(jnp.logical_not(native & (z == plane)))
         def _():
-            q_copy(t).wait_send()
-            st_copy(t).wait_send()
-            st_arrival(t).wait_recv()
-
-    each(blocks, settle)
-
-    def settle_plane(z):
-        @pl.when(z != plane)
-        def _():
-            kv_column(z).wait_send()
+            kv_land(z).wait_send()
             g_column(0, z).wait_send()
             g_column(1, z).wait_send()
 
-        def one(r):
-            kv_pass(z, r).wait_send()
-            g_pass(0, z, r).wait_send()
-            g_pass(1, z, r).wait_send()
-
-        spots_but_mine(one)
+        kv_across(z).wait_send()
+        kv_share(landed_block(z), z).wait_send()
+        kv_share(crossed_block(z), planes + z).wait_send()
 
     each(planes, settle_plane)
+
+    @pl.when(native)
+    def _():
+        w_copy().wait_send()
+
+        def relayed(n):
+            j = (n // 2) * group + 2 * column + n % 2
+            for d in range(1, group):
+                g_pass(0, j, d).wait_send()
+                g_pass(1, j, d).wait_send()
+
+        each(2 * planes, relayed)
+
     swap.wait()
     entries = 2 * blocks * width * 2 * features
     total = jnp.sum(sq_ref[0] + sq_ref[1], keepdims=True)
-    inverse = 1.0 / jnp.sqrt(total / entries + 1e-06)
-
-    for b in range(blocks):
-        update_ref[b] = update_ref[b] * inverse
-
-
-def whole_head(qt, kvt, w):
-    blocks, length, width = qt.shape
-    planes = kvt.shape[0]
+    scale_ref[...] = jnp.broadcast_to(1.0 / jnp.sqrt(total / entries + 1e-06), (8, width))
+    scale_out = pltpu.make_async_copy(scale_ref, scale_hbm, out_sem.at[2])
+    scale_out.start()
+    student_out.wait()
+    grad_out.wait()
+    scale_out.wait()
+
+
+def finish_kernel(
+    student_hbm, grad_hbm, scale_hbm, student_out, update_out,
+    st_ref, grad_ref, scale_ref, update_ref, in_sem, out_sem,
+):
+    parts, blocks, features, width = grad_ref.shape
+    chunks = in_sem.shape[0] - 2
+    each_len = blocks // chunks
+    fetches = [
+        pltpu.make_async_copy(
+            grad_hbm.at[:, pl.ds(n * each_len, each_len)],
+            grad_ref.at[:, pl.ds(n * each_len, each_len)], in_sem.at[n],
+        )
+        for n in range(chunks)
+    ]
+    scale_in = pltpu.make_async_copy(scale_hbm, scale_ref, in_sem.at[chunks])
+    student_in = pltpu.make_async_copy(student_hbm, st_ref, in_sem.at[chunks + 1])
+    scale_in.start()
+    for fetch in fetches:
+        fetch.start()
+    student_in.start()
+    scale_in.wait()
+    scale = scale_ref[:1]
+    stores = []
+    for n, fetch in enumerate(fetches):
+        fetch.wait()
+        for j in range(n * each_len, (n + 1) * each_len):
+            piece = cat([grad_ref[0, j], grad_ref[1, j]], 0).astype(f32)
+            update_ref[j] = piece.T * scale
+        stores.append(
+            pltpu.make_async_copy(
+                update_ref.at[pl.ds(n * each_len, each_len)],
+                update_out.at[pl.ds(n * each_len, each_len)], out_sem.at[n],
+            )
+        )
+        stores[-1].start()
+    student_in.wait()
+    stores.append(pltpu.make_async_copy(st_ref, student_out, out_sem.at[chunks]))
+    stores[-1].start()
+    for store in stores:
+        store.wait()
+
+
+def whole_head(queries, keys, values, w):
+    length, blocks, width = queries.shape
+    planes = keys.shape[1]
     group = blocks // planes
-    double = w.shape[1]
+    double = w.shape[2]
+    half = double // 2
     rows, steps = 2 * length, blocks // 2
     vmem, dma = pltpu.VMEM, pltpu.SemaphoreType.DMA
-    return pl.pallas_call(
+    hbm = pl.BlockSpec(memory_space=pltpu.MemorySpace.HBM)
+    limit = 67_043_328
+    student, grads, scale = pl.pallas_call(
         head_kernel,
         out_shape=(
-            jax.ShapeDtypeStruct((blocks, length, width), bf16),
-            jax.ShapeDtypeStruct((blocks, width, double), f32),
+            jax.ShapeDtypeStruct((length, blocks, width), bf16),
+            jax.ShapeDtypeStruct((2, blocks, half, width), bf16),
+            jax.ShapeDtypeStruct((8, width), f32),
         ),
-        in_specs=[pl.BlockSpec(memory_space=vmem)] * 3,
-        out_specs=(pl.BlockSpec(memory_space=vmem),) * 2,
+        in_specs=[hbm] * 4,
+        out_specs=(hbm,) * 3,
         scratch_shapes=[
+            vmem((length, blocks, width), bf16),
+            vmem((length, planes, width), bf16),
+            vmem((length, planes, width), bf16),
+            vmem((width, double), f32),
+            vmem((blocks, length, width), bf16),
+            vmem((planes, 2, length, width), bf16),
             vmem((blocks, length, width), bf16),
             vmem((blocks, 2, length, width), bf16),
             vmem((blocks, length, width), bf16),
-            vmem((blocks, double // 2, width), bf16),
-            vmem((blocks, double // 2, width), bf16),
+            vmem((length, blocks, width), bf16),
+            vmem((blocks, length, width), bf16),
+            vmem((2, half, width), bf16),
+            vmem((2, blocks, half, width), bf16),
             vmem((2, 8, width), f32),
+            vmem((8, width), f32),
             vmem((blocks, double, width), f32),
             vmem((blocks, 1, double), f32),
             vmem((blocks, double, width), f32),
@@ -753,34 +919,54 @@
             dma((blocks,)),
             dma((planes,)),
             dma((blocks,)),
-            dma((planes, group)),
-            dma((2,)),
+            dma((planes,)),
+            dma((2 * planes,)),
+            dma((3,)),
             dma((blocks,)),
             dma((blocks,)),
             dma((2, planes)),
-            dma((2, planes, group)),
-            dma((blocks, 2)),
+            dma((2, blocks, group - 1)),
+            dma((2, blocks)),
             dma((1,)),
             dma((1,)),
+            dma((3,)),
+            dma((1,)),
+            dma((1,)),
+            dma((3,)),
         ],
         compiler_params=pltpu.CompilerParams(
-            vmem_limit_bytes=40 * 2**20, collective_id=0, has_side_effects=True
+            vmem_limit_bytes=limit, collective_id=0, has_side_effects=True
         ),
-    )(qt, kvt, w)
+    )(queries, keys, values, w)
+    chunks = 4
+    return pl.pallas_call(
+        finish_kernel,
+        out_shape=(
+            jax.ShapeDtypeStruct((length, blocks, width), bf16),
+            jax.ShapeDtypeStruct((blocks, width, double), f32),
+        ),
+        in_specs=[hbm] * 3,
+        out_specs=(hbm,) * 2,
+        scratch_shapes=[
+            vmem((length, blocks, width), bf16),
+            vmem((2, blocks, half, width), bf16),
+            vmem((8, width), f32),
+            vmem((blocks, width, double), f32),
+            dma((chunks + 2,)),
+            dma((chunks + 1,)),
+        ],
+        compiler_params=pltpu.CompilerParams(vmem_limit_bytes=limit),
+    )(student, grads, scale)
 
 
 def head_shards(queries, keys, values, feature_weight):
-    qt = jnp.transpose(queries, (1, 0, 2))
-    kvt = jnp.transpose(jnp.stack([keys, values]), (2, 0, 1, 3))
-    w = lax.dynamic_index_in_dim(feature_weight, lax.axis_index("ctx"), 0, False)
-    student, update = whole_head(qt, kvt, w)
-    return (jnp.transpose(student, (1, 0, 2)), update)
+    return whole_head(queries, keys, values, feature_weight)
 
 
 def shards(queries, keys, values, feature_weight):
     count = lax.axis_size("ctx")
     width = queries.shape[2]
-    fits = queries.shape[1] == count and lax.axis_size("head") == 2 and count % 4 == 0 and count * queries.shape[0] <= 4096
+    fits = queries.shape[1] == count and count == 4 * keys.shape[1] and lax.axis_size("head") == 2 and count % 4 == 0 and keys.shape[1] == 4 and count * queries.shape[0] <= 4096
     fits = fits and queries.shape[1] // keys.shape[1] % 4 == 0 and queries.shape[0] == width and feature_weight.shape[2] == width
     body = head_shards if fits else general_shards
     return body(queries, keys, values, feature_weight)

time: 59.6 us -> 54.9 us (0.921)
  local copies, waits for them, and re-layouts: 4.52 us -> 0 us
    unnamed x9 -> x0, local copies, waits for them, and re-layouts: 3.52 us -> none
    another operation x1 -> x0, local copies, waits for them, and re-layouts: 1 us -> none  [head_shards(): kvt = jnp.transpose(jnp.stack([keys, values]), (2, 0, 1, 3))]
    pallas_call x1 -> x2, Pallas kernels: 54.2 us -> 54.1 us  [the longest x1 51.8 us: whole_head(): pl.pallas_call(head_kernel, out_shape=(jax.ShapeDtypeStruct((length, bloc...]
where the time goes in v2:
time: 54.9 us; the launch traced here: 54.8 us
  Pallas kernels  54.1 us (99%)
  between operations  0.64 us (1%)
    pallas_call x1, Pallas kernels, whole_head(): pl.pallas_call(head_kernel, out_shape=(jax.ShapeDtypeStruct((length, bloc...  51.8 us
    pallas_call x1, Pallas kernels, whole_head(): pl.pallas_call(finish_kernel, out_shape=(jax.ShapeDtypeStruct((length, bl...  2.31 us

profile of v2, /device:TPU:0, one launch (start us, length us, event | category | flops | bytes accessed | tf_op | source)
XLA Modules:
  0.0 54.8 jit_solution(14561765137856068632)
XLA Ops:
  0.6 51.8 %shard_map.59 = (bf16[128,16,128]{2,1,0:T(8,128)(2,1)}, bf16[2,16,64,128]{3,2,1,0:T(8,128)(2,1)}, f32[8,128]{1,0:T(8,128)}) custom-call(bf16[128,16,128]{2,1,0:T(8,128)(2,1)} %q_hbm.1, bf16[128,4,128]{2,1,0:T(4,128)(2,1)} %k_hbm.1, bf16[128,4,128]{2,1,0:T(4,128)(2,1)} %v_hbm.1, f32[16,128,128]{2,1,0:T(8,128)} %w_hbm.1), custom_call_target="tpu_custom_call" | custom-call | tf_op jit(solution)/shard_map/pallas_call | solution.py:881
  52.4 2.3 %shard_map.60 = (bf16[128,16,128]{2,1,0:T(8,128)(2,1)}, f32[16,128,128]{2,1,0:T(8,128)}) custom-call(bf16[128,16,128]{2,1,0:T(8,128)(2,1)} %get-tuple-element.5.student_hbm, bf16[2,16,64,128]{3,2,1,0:T(8,128)(2,1)} %get-tuple-element.6.grad_hbm, f32[8,128]{1,0:T(8,128)} %get-tuple-element.7.scale_hbm), custom_call_target="tpu_custom_call" | custom-call | tf_op jit(solution)/shard_map/pallas_call | solution.py:942

commit v3 on v2

--- a/solution.py
+++ b/solution.py
@@ -547,16 +547,8 @@
     def push_turns(first, last):
         each((last - first) * group, lambda n: push(first * group + n))
 
+    push_turns(0, 1)
     land(0)
-    land(1)
-    cross(0)
-    push_turns(0, 1)
-    land(2)
-    cross(1)
-    land(3)
-    cross(2)
-    cross(3)
-
     @pl.when(native)
     def _():
         own_w.wait()
@@ -570,9 +562,19 @@
     wq_ref[...] = cat(split(cat([wq, -wq], 1), 3), 0)
     wk_ref[...] = cat(split(cat([wk, -wk], 1), 3), 0)
     gq_ref[...] = jnp.zeros_like(gq_ref)
-    push_turns(1, pairs)
-    for d in range(planes):
-        plane_keys(flip(plane, d))
+    land(1)
+    cross(0)
+    land(2)
+    cross(1)
+    land(3)
+    push_turns(1, 2)
+    plane_keys(flip(plane, 0))
+    cross(2)
+    plane_keys(flip(plane, 1))
+    cross(3)
+    push_turns(2, pairs)
+    plane_keys(flip(plane, 2))
+    plane_keys(flip(plane, 3))
 
     @pl.when(native)
     def _():
@@ -700,7 +702,10 @@
         ]
         for i, mix in zip(tokens, mixes):
             mix_ref[pl.ds(2 * i, 2)] = mix.astype(bf16).reshape(2, length, width)
-        each(4, lambda u: send_student(pair_block(p, u)))
+        @pl.when(turn < pairs - 1)
+        def _():
+            each(4, lambda u: send_student(pair_block(p, u)))
+
         mismatches = [mix - teacher for mix, teacher in zip(mixes, teachers)]
         g_nums = [x / den for x, den in zip(mismatches, dens)]
         g_dens = [
@@ -749,6 +754,7 @@
     gk = sum(backward(range(steps // 2)) + backward(range(steps // 2, steps - 1)))
     own_grad[1] = (gk[:features] - gk[features:]).astype(bf16)
     send_grad(1)
+    each(4, lambda u: send_student(pair_block((my_pair + pairs - 1) % pairs, u)))
     relay_grad(0)
     relay_grad(1)
 

time: 54.9 us -> 52.2 us (0.951)
  Pallas kernels: 54.1 us -> 51.4 us
    pallas_call x1, Pallas kernels: 51.8 us -> 49.1 us  [whole_head(): pl.pallas_call(head_kernel, out_shape=(jax.ShapeDtypeStruct((length, bloc...]
where the time goes in v3:
time: 52.2 us; the launch traced here: 52 us
  Pallas kernels  51.4 us (98%)
  between operations  0.64 us (1%)
    pallas_call x1, Pallas kernels, whole_head(): pl.pallas_call(head_kernel, out_shape=(jax.ShapeDtypeStruct((length, bloc...  49.1 us
    pallas_call x1, Pallas kernels, whole_head(): pl.pallas_call(finish_kernel, out_shape=(jax.ShapeDtypeStruct((length, bl...  2.31 us

profile of v3, /device:TPU:0, one launch (start us, length us, event | category | flops | bytes accessed | tf_op | source)
XLA Modules:
  0.0 52.0 jit_solution(16359757033055112958)
XLA Ops:
  0.6 49.1 %shard_map.59 = (bf16[128,16,128]{2,1,0:T(8,128)(2,1)}, bf16[2,16,64,128]{3,2,1,0:T(8,128)(2,1)}, f32[8,128]{1,0:T(8,128)}) custom-call(bf16[128,16,128]{2,1,0:T(8,128)(2,1)} %q_hbm.1, bf16[128,4,128]{2,1,0:T(4,128)(2,1)} %k_hbm.1, bf16[128,4,128]{2,1,0:T(4,128)(2,1)} %v_hbm.1, f32[16,128,128]{2,1,0:T(8,128)} %w_hbm.1), custom_call_target="tpu_custom_call" | custom-call | tf_op jit(solution)/shard_map/pallas_call | solution.py:887
  49.7 2.3 %shard_map.60 = (bf16[128,16,128]{2,1,0:T(8,128)(2,1)}, f32[16,128,128]{2,1,0:T(8,128)}) custom-call(bf16[128,16,128]{2,1,0:T(8,128)(2,1)} %get-tuple-element.5.student_hbm, bf16[2,16,64,128]{3,2,1,0:T(8,128)(2,1)} %get-tuple-element.6.grad_hbm, f32[8,128]{1,0:T(8,128)} %get-tuple-element.7.scale_hbm), custom_call_target="tpu_custom_call" | custom-call | tf_op jit(solution)/shard_map/pallas_call | solution.py:948

commit v4 on v3

--- a/solution.py
+++ b/solution.py
@@ -291,10 +291,10 @@
 def head_kernel(
     q_hbm, k_hbm, v_hbm, w_hbm, student_hbm, grad_hbm, scale_hbm,
     q_raw, k_raw, v_raw, w_ref, qt_ref, kvt_ref, q_all, kv_all, st_all, st_turned, mix_ref,
-    own_grad, gat_ref, sq_ref, scale_ref, own_ref, sum_ref, pre_ref, pre_norm_ref,
+    own_grad, gat_ref, sq_own, sq_all, sq_ref, scale_ref, own_ref, sum_ref, pre_ref, pre_norm_ref,
     score_ref, near_ref, kfeat_ref, gstate_ref, gnorm_ref, wq_ref, wk_ref, gq_ref,
-    q_send, q_recv, kv_send, kv_recv, kv_cross, kv_sibling, local_sem, st_send, st_recv,
-    g_send, g_relay, g_recv, sq_send, sq_recv, fetch_sem, w_send, w_recv, out_sem,
+    q_sem, kv_send, kv_recv, local_sem, st_sem, g_send, g_recv, g_final, sq_sem, fetch_sem,
+    w_send, w_recv, out_sem, swap_sem,
 ):
     blocks, length, width = qt_ref.shape
     planes = kvt_ref.shape[0]
@@ -327,14 +327,14 @@
         def _():
             greet(t, row)
 
-    each(blocks, greet_side)
-    each(blocks // 2, lambda n: greet((n // 2) * group + 2 * side + n % 2, 1 - row))
     fetches = [
         pltpu.make_async_copy(src, dst, fetch_sem.at[n])
         for n, (src, dst) in enumerate([(k_hbm, k_raw), (v_hbm, v_raw), (q_hbm, q_raw)])
     ]
     for fetch in fetches:
         fetch.start()
+    each(blocks, greet_side)
+    each(blocks // 2, lambda n: greet((n // 2) * group + 2 * side + n % 2, 1 - row))
     own_w = pltpu.make_async_copy(w_hbm.at[mine], w_ref, local_sem.at[2])
 
     @pl.when(native)
@@ -355,7 +355,7 @@
 
     def kv_land(g):
         return remote(
-            kvt_ref.at[g], kv_all.at[me], kv_send.at[g], kv_recv.at[me],
+            kvt_ref.at[g], kv_all.at[me], kv_send.at[0], kv_recv.at[plane],
             ctx=g * group + 2 * side + column, head=row,
         )
 
@@ -368,50 +368,51 @@
     def kv_across(z):
         block = landed_block(z)
         return remote(
-            kv_all.at[block], kv_all.at[block], kv_cross.at[z], kv_recv.at[block],
+            kv_all.at[block], kv_all.at[block], kv_send.at[1], kv_recv.at[planes + z],
             ctx=plane * group + 2 * row + 1 - column, head=side,
         )
 
-    def kv_share(block, n):
+    def kv_share(block, z):
         return remote(
-            kv_all.at[block], kv_all.at[block], kv_sibling.at[n], kv_recv.at[block],
+            kv_all.at[block], kv_all.at[block], kv_send.at[2], kv_recv.at[2 * planes + z],
             ctx=me, head=1 - side,
         )
 
     def q_copy(j):
         return remote(
-            qt_ref.at[j], q_all.at[me], q_send.at[j], q_recv.at[me],
+            qt_ref.at[j], q_all.at[me], q_sem.at[pairs], q_sem.at[my_pair],
             ctx=(j // group) * group + 2 * side + (j % group) // 2, head=j % 2,
         )
 
-    def q_arrival(b):
-        return remote(qt_ref.at[b], q_all.at[b], q_send.at[b], q_recv.at[b], ctx=b, head=row)
-
-    def kv_arrival(b):
-        return remote(kv_all.at[b], kv_all.at[b], kv_send.at[0], kv_recv.at[b], ctx=b, head=row)
+    def bulk(ref, send_sem, recv_sem):
+        return remote(ref, ref, send_sem, recv_sem, ctx=me, head=1 - side)
+
+    def kv_arrival(first, count, n):
+        return bulk(kv_all.at[pl.ds(first, count)], kv_send.at[0], kv_recv.at[n])
 
     def st_copy(b):
-        return remote(mix_ref.at[b], st_all.at[mine], st_send.at[b], st_recv.at[mine], ctx=b, head=row)
-
-    def st_arrival(j):
-        return remote(mix_ref.at[j], st_all.at[j], st_send.at[j], st_recv.at[j], ctx=j, head=row)
+        return remote(mix_ref.at[b], st_all.at[mine], st_sem.at[0], st_sem.at[1], ctx=b, head=row)
 
     def g_column(part, z):
         return remote(
-            own_grad.at[part], gat_ref.at[part, mine], g_send.at[part, z], g_recv.at[part, mine],
+            own_grad.at[part], gat_ref.at[part, mine], g_send.at[0], g_recv.at[part, 2 * plane + side],
             ctx=z * group + spot, head=row,
         )
 
     def g_pass(part, j, d):
         piece = gat_ref.at[part, j]
         return remote(
-            piece, piece, g_relay.at[part, j, d - 1], g_recv.at[part, j],
+            piece, piece, g_send.at[d], g_final.at[0],
             ctx=plane * group + flip(spot, d), head=side,
         )
 
-    def g_arrival(part, j):
-        piece = gat_ref.at[part, j]
-        return remote(piece, piece, g_send.at[part, 0], g_recv.at[part, j], ctx=j, head=row)
+    def g_landing(part, j, n):
+        return bulk(gat_ref.at[part, j], g_send.at[0], g_recv.at[part, n])
+
+    def sq_copy(t):
+        return remote(
+            sq_own, sq_all.at[mine], sq_sem.at[0], sq_sem.at[1], ctx=t, head=row
+        )
 
     def unless_own(b, body):
         @pl.when(jnp.logical_not(native & (b == me)))
@@ -461,28 +462,33 @@
     def land(d):
         z = flip(plane, d)
         block = landed_block(z)
-        unless_own(block, lambda: kv_arrival(block).wait_recv())
+        unless_own(block, lambda: kv_arrival(block, 1, z).wait_recv())
         kv_across(z).start()
         kv_share(block, z).start()
 
     def cross(d):
         z = flip(plane, d)
         block = crossed_block(z)
-        kv_arrival(block).wait_recv()
-        kv_share(block, planes + z).start()
+        kv_arrival(block, 1, planes + z).wait_recv()
+        kv_share(block, z).start()
 
     def load(part, i):
         if part == 0:
             return q_all[pl.ds(2 * i, 2)].reshape(rows, width)
         return kv_all[pl.ds(2 * i, 2), part - 1].reshape(rows, width)
 
-    def q_arrived(b):
-        unless_own(b, lambda: q_arrival(b).wait_recv())
-
-    def kv_arrived(b):
-        @pl.when((b % group) // 2 != side)
-        def _():
-            kv_arrival(b).wait_recv()
+    def either(less, body):
+        for flag, count in ((native, less), (jnp.logical_not(native), 0)):
+            @pl.when(flag)
+            def _():
+                body(count)
+
+    def q_arrived(p):
+        here = native & (p == my_pair)
+        for flag, count in ((here, 3), (jnp.logical_not(here), 4)):
+            @pl.when(flag)
+            def _():
+                bulk(q_all.at[pl.ds(0, count)], q_sem.at[pairs], q_sem.at[p]).wait_recv()
 
     def send_student(b):
         unless_own(b, lambda: st_copy(b).start())
@@ -514,13 +520,13 @@
 
                     @pl.when(j != mine)
                     def _():
-                        g_arrival(part, j).wait_recv()
+                        g_landing(part, j, 2 * flip(plane, z) + h).wait_recv()
 
                     for d in range(1, group):
                         g_pass(part, j, d).start()
 
     def key_side(pair):
-        each(4, lambda u: kv_arrived(4 * pair + u))
+        kv_arrival(group * pair, 2, 2 * planes + pair).wait_recv()
         steps_of = (2 * pair, 2 * pair + 1)
         ks, vs = ([load(part, i) for i in steps_of] for part in (1, 2))
         kfs = [
@@ -547,7 +553,6 @@
     def push_turns(first, last):
         each((last - first) * group, lambda n: push(first * group + n))
 
-    push_turns(0, 1)
     land(0)
     @pl.when(native)
     def _():
@@ -563,6 +568,7 @@
     wk_ref[...] = cat(split(cat([wk, -wk], 1), 3), 0)
     gq_ref[...] = jnp.zeros_like(gq_ref)
     land(1)
+    push_turns(0, 1)
     cross(0)
     land(2)
     cross(1)
@@ -593,7 +599,7 @@
     def forward(turn, carry):
         p = (my_pair + turn) % pairs
         a, b = 2 * p, steps - 1 - 2 * p
-        each(4, lambda u: q_arrived(pair_block(p, u)))
+        q_arrived(p)
         tokens = (a, b)
         qs = [load(0, i) for i in tokens]
         vs = [load(2, i) for i in tokens]
@@ -754,72 +760,41 @@
     gk = sum(backward(range(steps // 2)) + backward(range(steps // 2, steps - 1)))
     own_grad[1] = (gk[:features] - gk[features:]).astype(bf16)
     send_grad(1)
+    square = own_grad[...].astype(f32).reshape(2 * features, width)
+    sq_own[...] = jnp.sum(square * square, axis=0, keepdims=True)
+    each(blocks, lambda n: unless_own((me + n) % blocks, lambda: sq_copy((me + n) % blocks).start()))
+
+    @pl.when(native)
+    def _():
+        sq_all[mine] = sq_own[...]
+
     each(4, lambda u: send_student(pair_block((my_pair + pairs - 1) % pairs, u)))
     relay_grad(0)
     relay_grad(1)
 
-    def unless_mine(j, body):
-        @pl.when(jnp.logical_not(native & (j == mine)))
-        def _():
-            body()
-
-    each(blocks, lambda j: unless_mine(j, lambda: st_arrival(j).wait_recv()))
+    either(1, lambda n: bulk(st_all.at[pl.ds(0, blocks - n)], st_sem.at[0], st_sem.at[1]).wait_recv())
     st_turned[...] = jnp.transpose(st_all[...], (1, 0, 2))
     student_out = pltpu.make_async_copy(st_turned, student_hbm, out_sem.at[0])
     student_out.start()
 
-    def gathered(j):
-        relayed = native & ((j % group) // 2 == column)
-
-        @pl.when(jnp.logical_not(relayed))
-        def _():
-            g_arrival(0, j).wait_recv()
-            g_arrival(1, j).wait_recv()
-
-    each(blocks, gathered)
-    grad_out = pltpu.make_async_copy(gat_ref, grad_hbm, out_sem.at[1])
-    grad_out.start()
-    squares = jnp.zeros((8, width), f32)
-    for j in range(blocks):
-        piece = cat([gat_ref[0, j], gat_ref[1, j]], 0).astype(f32)
-        piece = piece.reshape(2 * features // 8, 8, width)
-        squares = squares + jnp.sum(piece * piece, axis=0)
-    sq_ref[0] = squares
+    either(1, lambda n: bulk(sq_all.at[pl.ds(0, blocks - n)], sq_sem.at[0], sq_sem.at[1]).wait_recv())
+    sq_ref[0] = jnp.sum(sq_all[...], axis=0)
     swap = remote(
-        sq_ref.at[0], sq_ref.at[1], sq_send.at[0], sq_recv.at[0], ctx=me, head=1 - side
+        sq_ref.at[0], sq_ref.at[1], swap_sem.at[0], swap_sem.at[1], ctx=me, head=1 - side
     )
     swap.start()
 
-    def settle(j):
-        unless_mine(j, lambda: q_copy(j).wait_send())
-        unless_own(j, lambda: st_copy(j).wait_send())
-
-    each(blocks, settle)
-
-    def settle_plane(z):
-        @pl.when(jnp.logical_not(native & (z == plane)))
-        def _():
-            kv_land(z).wait_send()
-            g_column(0, z).wait_send()
-            g_column(1, z).wait_send()
-
-        kv_across(z).wait_send()
-        kv_share(landed_block(z), z).wait_send()
-        kv_share(crossed_block(z), planes + z).wait_send()
-
-    each(planes, settle_plane)
+    either(1, lambda n: bulk(qt_ref.at[pl.ds(0, blocks - n)], q_sem.at[pairs], q_sem.at[0]).wait_send())
+    either(1, lambda n: bulk(mix_ref.at[pl.ds(0, blocks - n)], st_sem.at[0], st_sem.at[1]).wait_send())
+    either(1, lambda n: bulk(sq_all.at[pl.ds(0, blocks - n)], sq_sem.at[0], sq_sem.at[1]).wait_send())
+    either(1, lambda n: bulk(kvt_ref.at[pl.ds(0, planes - n)], kv_send.at[0], kv_recv.at[0]).wait_send())
+    bulk(kv_all.at[pl.ds(0, planes)], kv_send.at[1], kv_recv.at[0]).wait_send()
+    bulk(kv_all.at[pl.ds(0, 2 * planes)], kv_send.at[2], kv_recv.at[0]).wait_send()
+    either(2, lambda n: bulk(gat_ref.at[0, pl.ds(0, 2 * planes - n)], g_send.at[0], g_final.at[0]).wait_send())
 
     @pl.when(native)
     def _():
         w_copy().wait_send()
-
-        def relayed(n):
-            j = (n // 2) * group + 2 * column + n % 2
-            for d in range(1, group):
-                g_pass(0, j, d).wait_send()
-                g_pass(1, j, d).wait_send()
-
-        each(2 * planes, relayed)
 
     swap.wait()
     entries = 2 * blocks * width * 2 * features
@@ -827,9 +802,26 @@
     scale_ref[...] = jnp.broadcast_to(1.0 / jnp.sqrt(total / entries + 1e-06), (8, width))
     scale_out = pltpu.make_async_copy(scale_ref, scale_hbm, out_sem.at[2])
     scale_out.start()
+
+    @pl.when(native)
+    def _():
+        bulk(gat_ref.at[0], g_send.at[0], g_final.at[0]).wait_recv()
+
+    @pl.when(jnp.logical_not(native))
+    def _():
+        bulk(gat_ref, g_send.at[0], g_final.at[0]).wait_recv()
+
+    grad_out = pltpu.make_async_copy(gat_ref, grad_hbm, out_sem.at[1])
+    grad_out.start()
+
+    @pl.when(native)
+    def _():
+        for d in range(1, group):
+            bulk(gat_ref.at[0], g_send.at[d], g_final.at[0]).wait_send()
+
     student_out.wait()
+    scale_out.wait()
     grad_out.wait()
-    scale_out.wait()
 
 
 def finish_kernel(
@@ -907,7 +899,9 @@
             vmem((blocks, length, width), bf16),
             vmem((2, half, width), bf16),
             vmem((2, blocks, half, width), bf16),
-            vmem((2, 8, width), f32),
+            vmem((1, width), f32),
+            vmem((blocks, 1, width), f32),
+            vmem((2, 1, width), f32),
             vmem((8, width), f32),
             vmem((blocks, double, width), f32),
             vmem((blocks, 1, double), f32),
@@ -921,24 +915,20 @@
             vmem((3 * width, double), bf16),
             vmem((3 * width, double), bf16),
             vmem((double, width), f32),
-            dma((blocks,)),
-            dma((blocks,)),
-            dma((planes,)),
-            dma((blocks,)),
-            dma((planes,)),
-            dma((2 * planes,)),
+            dma((blocks // 4 + 1,)),
             dma((3,)),
-            dma((blocks,)),
-            dma((blocks,)),
-            dma((2, planes)),
-            dma((2, blocks, group - 1)),
-            dma((2, blocks)),
+            dma((3 * planes,)),
+            dma((3,)),
+            dma((2,)),
+            dma((group,)),
+            dma((2, 2 * planes)),
             dma((1,)),
-            dma((1,)),
+            dma((2,)),
             dma((3,)),
             dma((1,)),
             dma((1,)),
             dma((3,)),
+            dma((2,)),
         ],
         compiler_params=pltpu.CompilerParams(
             vmem_limit_bytes=limit, collective_id=0, has_side_effects=True

time: 52.2 us -> 49.1 us (0.941)
  Pallas kernels: 51.4 us -> 48 us
    pallas_call x1, Pallas kernels: 49.1 us -> 45.7 us  [whole_head(): pl.pallas_call(head_kernel, out_shape=(jax.ShapeDtypeStruct((length, bloc...]
where the time goes in v4:
time: 49.1 us; the launch traced here: 48.6 us
  Pallas kernels  48 us (98%)
  between operations  0.64 us (1%)
    pallas_call x1, Pallas kernels, whole_head(): pl.pallas_call(head_kernel, out_shape=(jax.ShapeDtypeStruct((length, bloc...  45.7 us
    pallas_call x1, Pallas kernels, whole_head(): pl.pallas_call(finish_kernel, out_shape=(jax.ShapeDtypeStruct((length, bl...  2.31 us

profile of v4, /device:TPU:0, one launch (start us, length us, event | category | flops | bytes accessed | tf_op | source)
XLA Modules:
  0.0 48.6 jit_solution(1138358350190994459)
XLA Ops:
  0.6 45.7 %shard_map.59 = (bf16[128,16,128]{2,1,0:T(8,128)(2,1)}, bf16[2,16,64,128]{3,2,1,0:T(8,128)(2,1)}, f32[8,128]{1,0:T(8,128)}) custom-call(bf16[128,16,128]{2,1,0:T(8,128)(2,1)} %q_hbm.1, bf16[128,4,128]{2,1,0:T(4,128)(2,1)} %k_hbm.1, bf16[128,4,128]{2,1,0:T(4,128)(2,1)} %v_hbm.1, f32[16,128,128]{2,1,0:T(8,128)} %w_hbm.1), custom_call_target="tpu_custom_call" | custom-call | tf_op jit(solution)/shard_map/pallas_call | solution.py:879
  46.3 2.3 %shard_map.60 = (bf16[128,16,128]{2,1,0:T(8,128)(2,1)}, f32[16,128,128]{2,1,0:T(8,128)}) custom-call(bf16[128,16,128]{2,1,0:T(8,128)(2,1)} %get-tuple-element.5.student_hbm, bf16[2,16,64,128]{3,2,1,0:T(8,128)(2,1)} %get-tuple-element.6.grad_hbm, f32[8,128]{1,0:T(8,128)} %get-tuple-element.7.scale_hbm), custom_call_target="tpu_custom_call" | custom-call | tf_op jit(solution)/shard_map/pallas_call | solution.py:938

commit v5 on v4

--- a/solution.py
+++ b/solution.py
@@ -250,12 +250,8 @@
     return mxu(cat(split(a, 2), dims[0][0][0]), cat([b, b], dims[0][1][0]), dims)
 
 
-def wide_by_wide(a, b, dims):
-    a_hi, a_lo = split(a, 2)
-    b_hi, b_lo = split(b, 2)
-    return mxu(
-        cat([a_hi, a_hi, a_lo], dims[0][0][0]), cat([b_hi, b_lo, b_hi], dims[0][1][0]), dims
-    )
+def wide_by_rounded(a, b, dims):
+    return wide_by_exact(a, b.astype(bf16), dims)
 
 
 def half_sum(x, halves):
@@ -293,7 +289,7 @@
     q_raw, k_raw, v_raw, w_ref, qt_ref, kvt_ref, q_all, kv_all, st_all, st_turned, mix_ref,
     own_grad, gat_ref, sq_own, sq_all, sq_ref, scale_ref, own_ref, sum_ref, pre_ref, pre_norm_ref,
     score_ref, near_ref, kfeat_ref, gstate_ref, gnorm_ref, wq_ref, wk_ref, gq_ref,
-    q_sem, kv_send, kv_recv, local_sem, st_sem, g_send, g_recv, g_final, sq_sem, fetch_sem,
+    q_sem, kv_send, kv_recv, local_sem, st_sem, g_send, g_recv, g_hop, g_final, sq_sem, fetch_sem,
     w_send, w_recv, out_sem, swap_sem,
 ):
     blocks, length, width = qt_ref.shape
@@ -399,11 +395,19 @@
             ctx=z * group + spot, head=row,
         )
 
-    def g_pass(part, j, d):
+    def g_pass(part, z, h, d):
+        piece = gat_ref.at[part, z * group + 2 * column + h]
+        arrival = g_hop.at[part, z] if (d == 1) == (h == 0) else g_final.at[0]
+        return remote(
+            piece, piece, g_send.at[d], arrival, ctx=plane * group + flip(spot, d), head=side
+        )
+
+    def g_forward(part, z):
+        j = z * group + jnp.where(native, 2 - 2 * column, 2 * column + 1)
         piece = gat_ref.at[part, j]
+        target = jnp.where(native, flip(spot, 2), flip(spot, 1))
         return remote(
-            piece, piece, g_send.at[d], g_final.at[0],
-            ctx=plane * group + flip(spot, d), head=side,
+            piece, piece, g_send.at[3], g_final.at[0], ctx=plane * group + target, head=side
         )
 
     def g_landing(part, j, n):
@@ -522,8 +526,14 @@
                     def _():
                         g_landing(part, j, 2 * flip(plane, z) + h).wait_recv()
 
-                    for d in range(1, group):
-                        g_pass(part, j, d).start()
+                    for d in range(1, group - 1):
+                        g_pass(part, flip(plane, z), h, d).start()
+
+    def hop_grad(part):
+        for d in range(planes):
+            z = flip(plane, d)
+            bulk(gat_ref.at[part, z], g_send.at[0], g_hop.at[part, z]).wait_recv()
+            g_forward(part, z).start()
 
     def key_side(pair):
         kv_arrival(group * pair, 2, 2 * planes + pair).wait_recv()
@@ -697,7 +707,7 @@
             for i in tokens
         ]
         decays = [jnp.exp2(-top) for top in win_maxs]
-        fars = halves_of(lambda x, h: wide_by_wide(cut(qfs[x], h), states[x][h], NN))
+        fars = halves_of(lambda x, h: wide_by_rounded(cut(qfs[x], h), states[x][h], NN))
         dens = [
             win_den + decay * jnp.sum(qf * norm, axis=-1, keepdims=True)
             for win_den, decay, qf, norm in zip(win_dens, decays, qfs, norms)
@@ -722,9 +732,9 @@
         pulled_norms = [lift * g_den for lift, g_den in zip(lifts, g_dens)]
         for x, i in enumerate(tokens):
             for h in range(2):
-                gstate_ref[2 * i + h] = wide_by_wide(cut(lifts[x], h), cut(g_nums[x], h), TN)
+                gstate_ref[2 * i + h] = wide_by_rounded(cut(lifts[x], h), cut(g_nums[x], h), TN)
                 gnorm_ref[2 * i + h] = jnp.sum(cut(pulled_norms[x], h), axis=0, keepdims=True)
-        pulled = halves_of(lambda x, h: wide_by_wide(cut(g_nums[x], h), states[x][h], NT))
+        pulled = halves_of(lambda x, h: wide_by_rounded(cut(g_nums[x], h), states[x][h], NT))
         g_qfs = [
             decay * (pull + norm * g_den)
             for decay, pull, norm, g_den in zip(decays, pulled, norms, g_dens)
@@ -771,6 +781,8 @@
     each(4, lambda u: send_student(pair_block((my_pair + pairs - 1) % pairs, u)))
     relay_grad(0)
     relay_grad(1)
+    hop_grad(0)
+    hop_grad(1)
 
     either(1, lambda n: bulk(st_all.at[pl.ds(0, blocks - n)], st_sem.at[0], st_sem.at[1]).wait_recv())
     st_turned[...] = jnp.transpose(st_all[...], (1, 0, 2))
@@ -805,20 +817,21 @@
 
     @pl.when(native)
     def _():
-        bulk(gat_ref.at[0], g_send.at[0], g_final.at[0]).wait_recv()
+        bulk(gat_ref.at[0, pl.ds(0, 2 * planes)], g_send.at[0], g_final.at[0]).wait_recv()
 
     @pl.when(jnp.logical_not(native))
     def _():
-        bulk(gat_ref, g_send.at[0], g_final.at[0]).wait_recv()
+        bulk(gat_ref.at[:, pl.ds(0, 3 * planes)], g_send.at[0], g_final.at[0]).wait_recv()
 
     grad_out = pltpu.make_async_copy(gat_ref, grad_hbm, out_sem.at[1])
     grad_out.start()
 
     @pl.when(native)
     def _():
-        for d in range(1, group):
+        for d in range(1, group - 1):
             bulk(gat_ref.at[0], g_send.at[d], g_final.at[0]).wait_send()
 
+    bulk(gat_ref.at[0, pl.ds(0, 2 * planes)], g_send.at[3], g_final.at[0]).wait_send()
     student_out.wait()
     scale_out.wait()
     grad_out.wait()
@@ -841,12 +854,14 @@
     scale_in = pltpu.make_async_copy(scale_hbm, scale_ref, in_sem.at[chunks])
     student_in = pltpu.make_async_copy(student_hbm, st_ref, in_sem.at[chunks + 1])
     scale_in.start()
+    student_in.start()
     for fetch in fetches:
         fetch.start()
-    student_in.start()
     scale_in.wait()
     scale = scale_ref[:1]
-    stores = []
+    stores = [pltpu.make_async_copy(st_ref, student_out, out_sem.at[chunks])]
+    student_in.wait()
+    stores[0].start()
     for n, fetch in enumerate(fetches):
         fetch.wait()
         for j in range(n * each_len, (n + 1) * each_len):
@@ -859,9 +874,6 @@
             )
         )
         stores[-1].start()
-    student_in.wait()
-    stores.append(pltpu.make_async_copy(st_ref, student_out, out_sem.at[chunks]))
-    stores[-1].start()
     for store in stores:
         store.wait()
 
@@ -922,6 +934,7 @@
             dma((2,)),
             dma((group,)),
             dma((2, 2 * planes)),
+            dma((2, planes)),
             dma((1,)),
             dma((2,)),
             dma((3,)),
@@ -934,7 +947,7 @@
             vmem_limit_bytes=limit, collective_id=0, has_side_effects=True
         ),
     )(queries, keys, values, w)
-    chunks = 4
+    chunks = 2
     return pl.pallas_call(
         finish_kernel,
         out_shape=(

time: 49.1 us -> 48.7 us (level)
  no operation moved by 1% of the time
where the time goes in v5:
time: 48.7 us; the launch traced here: 48.4 us
  Pallas kernels  47.8 us (98%)
  between operations  0.64 us (1%)
    pallas_call x1, Pallas kernels, whole_head(): pl.pallas_call(head_kernel, out_shape=(jax.ShapeDtypeStruct((length, bloc...  45.5 us
    pallas_call x1, Pallas kernels, whole_head(): pl.pallas_call(finish_kernel, out_shape=(jax.ShapeDtypeStruct((length, bl...  2.28 us

profile of v5, /device:TPU:0, one launch (start us, length us, event | category | flops | bytes accessed | tf_op | source)
XLA Modules:
  0.0 48.4 jit_solution(11602614008152032944)
XLA Ops:
  0.6 45.5 %shard_map.59 = (bf16[128,16,128]{2,1,0:T(8,128)(2,1)}, bf16[2,16,64,128]{3,2,1,0:T(8,128)(2,1)}, f32[8,128]{1,0:T(8,128)}) custom-call(bf16[128,16,128]{2,1,0:T(8,128)(2,1)} %q_hbm.1, bf16[128,4,128]{2,1,0:T(4,128)(2,1)} %k_hbm.1, bf16[128,4,128]{2,1,0:T(4,128)(2,1)} %v_hbm.1, f32[16,128,128]{2,1,0:T(8,128)} %w_hbm.1), custom_call_target="tpu_custom_call" | custom-call | tf_op jit(solution)/shard_map/pallas_call | solution.py:891
  46.1 2.3 %shard_map.60 = (bf16[128,16,128]{2,1,0:T(8,128)(2,1)}, f32[16,128,128]{2,1,0:T(8,128)}) custom-call(bf16[128,16,128]{2,1,0:T(8,128)(2,1)} %get-tuple-element.5.student_hbm, bf16[2,16,64,128]{3,2,1,0:T(8,128)(2,1)} %get-tuple-element.6.grad_hbm, f32[8,128]{1,0:T(8,128)} %get-tuple-element.7.scale_hbm), custom_call_target="tpu_custom_call" | custom-call | tf_op jit(solution)/shard_map/pallas_call | solution.py:951

commit v6 on v5

--- a/solution.py
+++ b/solution.py
@@ -756,7 +756,7 @@
         g_kfs = [
             cat(
                 [
-                    exact_by_wide(v[h * length:(h + 1) * length], gstate_ref[2 * i + h + 2], NT)
+                    mxu(v[h * length:(h + 1) * length], gstate_ref[2 * i + h + 2].astype(bf16), NT)
                     + gnorm_ref[2 * i + h + 2]
                     for h in range(2)
                 ],

time: 48.7 us -> 48.8 us (level)
  no operation moved by 1% of the time
where the time goes in v6:
time: 48.8 us; the launch traced here: 48.4 us
  Pallas kernels  47.7 us (98%)
  between operations  0.64 us (1%)
    pallas_call x1, Pallas kernels, whole_head(): pl.pallas_call(head_kernel, out_shape=(jax.ShapeDtypeStruct((length, bloc...  45.4 us
    pallas_call x1, Pallas kernels, whole_head(): pl.pallas_call(finish_kernel, out_shape=(jax.ShapeDtypeStruct((length, bl...  2.28 us

profile of v6, /device:TPU:0, one launch (start us, length us, event | category | flops | bytes accessed | tf_op | source)
XLA Modules:
  0.0 48.4 jit_solution(10084238168006039756)
XLA Ops:
  0.6 45.4 %shard_map.59 = (bf16[128,16,128]{2,1,0:T(8,128)(2,1)}, bf16[2,16,64,128]{3,2,1,0:T(8,128)(2,1)}, f32[8,128]{1,0:T(8,128)}) custom-call(bf16[128,16,128]{2,1,0:T(8,128)(2,1)} %q_hbm.1, bf16[128,4,128]{2,1,0:T(4,128)(2,1)} %k_hbm.1, bf16[128,4,128]{2,1,0:T(4,128)(2,1)} %v_hbm.1, f32[16,128,128]{2,1,0:T(8,128)} %w_hbm.1), custom_call_target="tpu_custom_call" | custom-call | tf_op jit(solution)/shard_map/pallas_call | solution.py:891
  46.1 2.3 %shard_map.60 = (bf16[128,16,128]{2,1,0:T(8,128)(2,1)}, f32[16,128,128]{2,1,0:T(8,128)}) custom-call(bf16[128,16,128]{2,1,0:T(8,128)(2,1)} %get-tuple-element.5.student_hbm, bf16[2,16,64,128]{3,2,1,0:T(8,128)(2,1)} %get-tuple-element.6.grad_hbm, f32[8,128]{1,0:T(8,128)} %get-tuple-element.7.scale_hbm), custom_call_target="tpu_custom_call" | custom-call | tf_op jit(solution)/shard_map/pallas_call | solution.py:951

commit v7 on v6

--- a/solution.py
+++ b/solution.py
@@ -564,6 +564,7 @@
         each((last - first) * group, lambda n: push(first * group + n))
 
     land(0)
+    push_turns(0, 1)
     @pl.when(native)
     def _():
         own_w.wait()
@@ -578,7 +579,6 @@
     wk_ref[...] = cat(split(cat([wk, -wk], 1), 3), 0)
     gq_ref[...] = jnp.zeros_like(gq_ref)
     land(1)
-    push_turns(0, 1)
     cross(0)
     land(2)
     cross(1)

time: 48.8 us -> 48.7 us (level)
  no operation moved by 1% of the time
where the time goes in v7:
time: 48.7 us; the launch traced here: 48.4 us
  Pallas kernels  47.7 us (98%)
  between operations  0.64 us (1%)
    pallas_call x1, Pallas kernels, whole_head(): pl.pallas_call(head_kernel, out_shape=(jax.ShapeDtypeStruct((length, bloc...  45.5 us
    pallas_call x1, Pallas kernels, whole_head(): pl.pallas_call(finish_kernel, out_shape=(jax.ShapeDtypeStruct((length, bl...  2.28 us

profile of v7, /device:TPU:0, one launch (start us, length us, event | category | flops | bytes accessed | tf_op | source)
XLA Modules:
  0.0 48.4 jit_solution(8897100720782997531)
XLA Ops:
  0.6 45.5 %shard_map.59 = (bf16[128,16,128]{2,1,0:T(8,128)(2,1)}, bf16[2,16,64,128]{3,2,1,0:T(8,128)(2,1)}, f32[8,128]{1,0:T(8,128)}) custom-call(bf16[128,16,128]{2,1,0:T(8,128)(2,1)} %q_hbm.1, bf16[128,4,128]{2,1,0:T(4,128)(2,1)} %k_hbm.1, bf16[128,4,128]{2,1,0:T(4,128)(2,1)} %v_hbm.1, f32[16,128,128]{2,1,0:T(8,128)} %w_hbm.1), custom_call_target="tpu_custom_call" | custom-call | tf_op jit(solution)/shard_map/pallas_call | solution.py:891
  46.1 2.3 %shard_map.60 = (bf16[128,16,128]{2,1,0:T(8,128)(2,1)}, f32[16,128,128]{2,1,0:T(8,128)}) custom-call(bf16[128,16,128]{2,1,0:T(8,128)(2,1)} %get-tuple-element.5.student_hbm, bf16[2,16,64,128]{3,2,1,0:T(8,128)(2,1)} %get-tuple-element.6.grad_hbm, f32[8,128]{1,0:T(8,128)} %get-tuple-element.7.scale_hbm), custom_call_target="tpu_custom_call" | custom-call | tf_op jit(solution)/shard_map/pallas_call | solution.py:951
